TPU v7x, 32 devices: a whole 2x2x4 slice. The times are simulated.
32 devices in a mesh: grp: 2 (over x), wk: 16 (over z, y, core).
Axes of the slice: x: 2, y: 2, z: 4, core: 2. Of those that a mesh axis runs over, the one named last changes fastest.
Arguments:
- grads: bfloat16 [2, 4, 512, 1024], P('grp', None, 'wk'), may hold values from -4 to 4
- bank: bfloat16 [16, 5, 512, 512], P('wk'), as said below
- owners: int32 [4], replicated, may hold values from 0 to 15, as said below
- col_map: int32 [4, 2], replicated, may hold values from 0 to 3
Outputs:
- update: float32 [4, 512, 1024], P(None, 'grp', 'wk')
Inputs may be any that keep to these rules, and one draw needn't show every extreme that they name: `owners`: 4 distinct worker indices; the last worker serves one of the layers. `bank`: every block is symmetric.
All inputs are finite; a program needn't handle non-finite values.
Results may differ from a plain program's by a relative error of at most 0.015.
Values may be sent and summed in bfloat16 or wider, within the bound.
No kernel may reach another device: no remote copies, remote signals or barrier semaphores. Data moves between devices by JAX's collectives and lax.ppermute only.
A program may use at most 64 MiB of HBM per device.

v0:
```python
import jax
import jax.numpy as jnp
from jax import lax
from jax.sharding import PartitionSpec as P


def spread(value, axis, root):
    mine = lax.axis_index(axis) == root
    return lax.psum(jnp.where(mine, value, jnp.zeros_like(value)), axis)


def right_multiply(rows_in, right_blocks):
    rows_count = rows_in.shape[0]
    blocks = right_blocks.shape[0]
    block = right_blocks.shape[1]
    split_rows = rows_in.reshape(rows_count, blocks, block)
    mixed = jnp.einsum("nkb,kbc->nkc", split_rows, right_blocks, preferred_element_type=jnp.float32)
    return mixed.reshape(rows_count, blocks * block).astype(jnp.bfloat16)


def on_device(grads, bank, owners, col_map):
    layer_total = grads.shape[1]
    width_total = grads.shape[3]
    block = bank.shape[2]
    rows_output = block // lax.axis_size("grp")
    row_offset = lax.axis_index("grp") * rows_output
    col_count = width_total // lax.axis_size("wk")
    col_offset = lax.axis_index("wk") * col_count
    results = []
    for layer_index in range(layer_total):
        chosen = jnp.take(bank[0, 1:], col_map[layer_index], axis=0)
        selected = jnp.concatenate([bank[0, :1], chosen], axis=0)
        factors = spread(selected, "wk", owners[layer_index])
        left_inverse = factors[0]
        right_blocks = factors[1:]
        left_rows = lax.dynamic_slice_in_dim(left_inverse, row_offset, rows_output, 0)
        summed = lax.psum(grads[0, layer_index].astype(jnp.float32).astype(jnp.bfloat16), "grp")
        mixed_full = right_multiply(lax.all_gather(summed, "wk", axis=0, tiled=True), right_blocks)
        mixed_cols = lax.dynamic_slice_in_dim(mixed_full, col_offset, col_count, 1)
        output_rows = jnp.dot(left_rows, mixed_cols, preferred_element_type=jnp.float32)
        results.append(output_rows)
    return jnp.stack(results)


def solution(mesh):
    in_specs = (P("grp", None, "wk", None), P("wk", None, None, None), P(), P())
    out_specs = P(None, "grp", "wk")
    return jax.shard_map(
        on_device, mesh=mesh, in_specs=in_specs, out_specs=out_specs, check_vma=False
    )
```

profile of v0, /device:TPU:0, one launch (start us, length us, event | category | flops | bytes accessed | tf_op | source)
XLA Modules:
  0.0 350.5 jit_solution(1073595287324214418)
XLA Ops:
  6.5 1.6 slice_bitcast_fusion.4
  8.2 27.8 %all-reduce.7.cloned.1.call-done = (bf16[32,1024]{1,0:T(8,128)(2,1)}, bf16[32,1024]{1,0:T(8,128)(2,1)}, bf16[32,1024]{1,0:T(8,128)(2,1)}, bf16[32,1024]{1,0:T(8,128)(2,1)}) async-done(((bf16[32,1024]{1,0:T(8,128)(2,1)}, bf16[32,1024]{1,0:T(8,128)(2,1)}, bf16[32,1024]{1,0:T(8,128)(2,1)}, bf16[32,1024]{1,0:T(8,128)(2,1)}), (bf16[32,1024]{1,0:T(8,128)(2,1)}, bf16[32,1024]{1,0:T(8,128)(2,1)}, ...) | async-done | bytes 262160 | tf_op jit(solution)/shard_map/psum | solution.py:37
  37.4 1.0 slice_reduce_fusion.3
  38.5 1.5 fusion.20
  39.9 1.7 slice_bitcast_fusion
  41.8 1.9 slice.73
  43.6 1.6 gather_fusion.3
  45.2 1.5 copy.29
  46.7 1.6 gather_fusion.2
  48.3 2.3 copy.26
  50.6 1.6 gather_fusion.1
  52.2 2.3 copy.23
  54.5 1.6 gather_fusion
  56.1 1.5 copy.20
  60.1 2.1 copy.36
  62.6 1.0 copy-done.1
  64.0 0.9 copy-done.2
  64.9 3.0 fusion
  67.9 8.2 %all-gather.5.cloned.1.call-done = bf16[512,1024]{1,0:T(8,128)(2,1)} async-done(((bf16[32,1024]{1,0:T(8,128)(2,1)}), bf16[512,1024]{1,0:T(8,128)(2,1)}) %all-gather.5.cloned.1.call-update) | async-done | bytes 1048592 | tf_op jit(solution)/shard_map/all_gather | solution.py:38
  76.1 1.5 copy.21
  77.6 37.5 %all-gather.7.cloned.1.call-done = bf16[512,1024]{1,0:T(8,128)(2,1)} async-done(((bf16[32,1024]{1,0:T(8,128)(2,1)}), bf16[512,1024]{1,0:T(8,128)(2,1)}) %all-gather.7.cloned.1.call-update) | async-done | bytes 1048592 | tf_op jit(solution)/shard_map/all_gather | solution.py:38
  115.1 1.5 copy.24
  116.6 37.4 %all-gather.9.cloned.1.call-done = bf16[512,1024]{1,0:T(8,128)(2,1)} async-done(((bf16[32,1024]{1,0:T(8,128)(2,1)}), bf16[512,1024]{1,0:T(8,128)(2,1)}) %all-gather.9.cloned.1.call-update) | async-done | bytes 1048592 | tf_op jit(solution)/shard_map/all_gather | solution.py:38
  154.0 1.5 copy.27
  155.5 37.4 %all-gather.11.cloned.1.call-done = bf16[512,1024]{1,0:T(8,128)(2,1)} async-done(((bf16[32,1024]{1,0:T(8,128)(2,1)}), bf16[512,1024]{1,0:T(8,128)(2,1)}) %all-gather.11.cloned.1.call-update) | async-done | bytes 1048592 | tf_op jit(solution)/shard_map/all_gather | solution.py:38
  192.9 2.3 copy.30
  195.2 139.9 %all-reduce.5.cloned.1.call-done = (bf16[3,512,512]{1,2,0:T(8,128)(2,1)}, bf16[3,512,512]{1,2,0:T(8,128)(2,1)}, bf16[3,512,512]{1,2,0:T(8,128)(2,1)}, bf16[3,512,512]{1,2,0:T(8,128)(2,1)}) async-done(((bf16[3,512,512]{1,2,0:T(8,128)(2,1)}, bf16[3,512,512]{1,2,0:T(8,128)(2,1)}, bf16[3,512,512]{1,2,0:T(8,128)(2,1)}, bf16[3,512,512]{1,2,0:T(8,128)(2,1)}), (bf16[3,512,512]{1,2,0:T(8,128)(2,1)}, ...) | async-done | bytes 6291472 | tf_op jit(solution)/shard_map/psum | solution.py:9
  335.1 1.1 slice.102
  336.2 2.1 convolution_convert_fusion.3
  338.3 0.7 convolution_convert_fusion.2
  339.8 0.7 convolution_convert_fusion.1
  342.9 0.7 pad_maximum_fusion.4
  (44 shorter events, 5.3 us)
Async XLA Ops:
  6.5 29.4 %all-reduce.7.cloned.1.call-start = ((), (), s32[]{:S(2)}) async-start(), calls=%async_computation.5 | async-start | bytes 524288 | tf_op jit(solution)/shard_map/psum | solution.py:37
  8.2 67.9 %all-gather.5.cloned.1.call-start = ((), (), s32[]{:S(2)}) async-start(), calls=%async_computation | async-start | bytes 1114112 | tf_op jit(solution)/shard_map/all_gather | solution.py:38
  36.0 79.1 %all-gather.7.cloned.1.call-start = ((), (), s32[]{:S(2)}) async-start(), calls=%async_computation.1 | async-start | bytes 1114112 | tf_op jit(solution)/shard_map/all_gather | solution.py:38
  36.7 117.3 %all-gather.9.cloned.1.call-start = ((), (), s32[]{:S(2)}) async-start(), calls=%async_computation.2 | async-start | bytes 1114112 | tf_op jit(solution)/shard_map/all_gather | solution.py:38
  37.3 155.6 %all-gather.11.cloned.1.call-start = ((), (), s32[]{:S(2)}) async-start(), calls=%async_computation.3 | async-start | bytes 1114112 | tf_op jit(solution)/shard_map/all_gather | solution.py:38
  41.7 293.4 %all-reduce.5.cloned.1.call-start = ((), (), s32[]{:S(2)}) async-start(), calls=%async_computation.4 | async-start | bytes 12582912 | tf_op jit(solution)/shard_map/psum | solution.py:9
  60.1 2.4 copy-start
  62.4 1.2 copy-start.1
  63.8 1.0 copy-start.2
  336.2 2.1 copy-start.6
  338.3 1.4 copy-start.5
  339.8 1.4 copy-start.4
  339.8 1.7 copy-start.3
Sparse Core Ops, SparseCore 0:
  9.8 26.1 all-reduce.6
  38.1 37.8 all-gather.4
  78.2 36.8 all-gather.6
  117.1 36.8 all-gather.8
  156.0 36.8 all-gather.10
  196.7 138.3 all-reduce.4
where the time goes:
time: 351 us; the launch traced here: 350 us
  waiting for transfers between devices  289 us (82%)
  local copies, waits for them, and re-layouts  35.2 us (10%)
  between operations  16.2 us (5%)
  matrix products  4.9 us (1%)
  other arithmetic  4.43 us (1%)
    psum x1, waiting for transfers between devices, spread(): return lax.psum(jnp.where(mine, value, jnp.zeros_like(value)), axis)  140 us
    all_gather x4, waiting for transfers between devices, on_device(): lax.all_gather(summed, 'wk', axis=0, tiled=True)  120 us
    psum x1, waiting for transfers between devices, on_device(): lax.psum(grads[0, layer_index].astype(jnp.float32).astype(jnp.bfloat16),...  27.8 us
    gather x8, local copies, waits for them, and re-layouts, on_device(): chosen = jnp.take(bank[0, 1:], col_map[layer_index], axis=0)  13.9 us
  transfers between devices with their start and end apart: 6, of which 6 were waited for; matrix products, arithmetic and copies ran while one was open for 9% of the time, Pallas kernels for 0%

commit v1 on v0

v1 whole, which is shorter than its diff:
```python
import jax
import jax.numpy as jnp
from jax import lax
from jax.sharding import PartitionSpec as P


def shifted(value, axis, shift):
    size = lax.axis_size(axis)
    return lax.ppermute(value, axis, [(i, (i + shift) % size) for i in range(size)])


def summed_columns(rows, axis):
    groups = lax.axis_size(axis)
    me = lax.axis_index(axis)
    width = rows.shape[-1] // groups

    def columns(index):
        return lax.dynamic_slice_in_dim(rows, index * width, width, rows.ndim - 1)

    total = columns(me).astype(jnp.float32)
    for shift in range(1, groups):
        total += shifted(columns((me + shift) % groups), axis, shift).astype(jnp.float32)
    return total.astype(jnp.bfloat16)


def swap_rows_for_columns(columns_by_rows, axis):
    groups = lax.axis_size(axis)
    me = lax.axis_index(axis)
    columns, rows = columns_by_rows.shape
    share = rows // groups

    def piece(index):
        return lax.dynamic_slice_in_dim(columns_by_rows, index * share, share, 1)

    full = jnp.zeros((groups * columns, share), columns_by_rows.dtype)
    for shift in range(groups):
        sent = piece((me + shift) % groups)
        got = shifted(sent, axis, shift) if shift else sent
        full = lax.dynamic_update_slice_in_dim(full, got, ((me - shift) % groups) * columns, 0)
    return full


def on_device(grads, bank, owners, col_map):
    layers = grads.shape[1]
    block = bank.shape[2]
    workers = lax.axis_size("wk")
    worker = lax.axis_index("wk")

    summed = summed_columns(grads[0], "grp")

    serves = owners[None, :] == jnp.arange(workers, dtype=owners.dtype)[:, None]
    outgoing = jnp.zeros((workers,) + summed.shape[1:], summed.dtype)
    for layer in range(layers):
        outgoing = jnp.where(serves[:, layer, None, None], summed[layer][None], outgoing)
    gathered = lax.all_to_all(outgoing, "wk", 0, 0, tiled=True).reshape(block, -1)

    my_layer = jnp.sum(jnp.where(owners == worker, jnp.arange(layers), 0))
    left = bank[0, 0]
    left_product = lax.dot_general(
        gathered, left, (((0,), (0,)), ((), ())), preferred_element_type=jnp.float32
    ).astype(jnp.bfloat16)
    left_product = swap_rows_for_columns(left_product, "grp")
    pieces = []
    for index in range(col_map.shape[1]):
        right = lax.dynamic_index_in_dim(bank[0], 1 + col_map[my_layer, index], 0, False)
        part = left_product[index * block : (index + 1) * block]
        pieces.append(jnp.dot(right, part, preferred_element_type=jnp.float32).astype(jnp.bfloat16))
    product = jnp.concatenate(pieces, axis=0)

    product = product.reshape(workers, -1, product.shape[1])
    returned = lax.all_to_all(product, "wk", 0, 0, tiled=True)
    results = []
    for layer in range(layers):
        part = lax.dynamic_index_in_dim(returned, owners[layer], 0, False)
        results.append(part.astype(jnp.float32).T)
    return jnp.stack(results)


def solution(mesh):
    in_specs = (P("grp", None, "wk", None), P("wk", None, None, None), P(), P())
    out_specs = P(None, "grp", "wk")
    return jax.shard_map(
        on_device, mesh=mesh, in_specs=in_specs, out_specs=out_specs, check_vma=False
    )
```

time: 351 us -> 63.6 us (0.18)
  waiting for transfers between devices: 289 us -> 24 us
  local copies, waits for them, and re-layouts: 35.2 us -> 2.37 us
  starting transfers between devices: 0.2 us -> 15.2 us
  between operations: 16.2 us -> 12.3 us
    psum x2 -> x0, waiting for transfers between devices: 168 us -> none  [the longest x1 140 us: spread(): return lax.psum(jnp.where(mine, value, jnp.zeros_like(value)), axis)]
    all_gather x4 -> x0, waiting for transfers between devices: 120 us -> none  [on_device(): lax.all_gather(summed, 'wk', axis=0, tiled=True)]
    all_to_all x0 -> x2, waiting for transfers between devices: none -> 20.2 us  [the longest x1 14.2 us: on_device(): lax.all_to_all(outgoing, 'wk', 0, 0, tiled=True).reshape(block, -1)]
    gather x8 -> x0, local copies, waits for them, and re-layouts: 13.9 us -> none  [on_device(): chosen = jnp.take(bank[0, 1:], col_map[layer_index], axis=0)]
    all_to_all x0 -> x2, starting transfers between devices: none -> 10.6 us  [the longest x1 6.19 us: on_device(): lax.all_to_all(outgoing, 'wk', 0, 0, tiled=True).reshape(block, -1)]
    all_gather x4 -> x0, local copies, waits for them, and re-layouts: 6.76 us -> none  [on_device(): lax.all_gather(summed, 'wk', axis=0, tiled=True)]
    unnamed x15 -> x4, local copies, waits for them, and re-layouts: 5.65 us -> 0.01 us
    slice x7 -> x1, local copies, waits for them, and re-layouts: 5.55 us -> 0.65 us  [on_device(): part = lax.dynamic_index_in_dim(returned, owners[layer], 0, False)]
  transfers between devices with their start and end apart: 6 -> 4, of which waited for: 6 -> 4; matrix products, arithmetic and copies ran while one was open for 9% -> 4% of each run, Pallas kernels for 0% -> 0%
where the time goes in v1:
time: 63.6 us; the launch traced here: 62.9 us
  waiting for transfers between devices  24 us (38%)
  starting transfers between devices  15.2 us (24%)
  between operations  12.3 us (19%)
  other arithmetic  4.83 us (8%)
  matrix products  4.19 us (7%)
  local copies, waits for them, and re-layouts  2.37 us (4%)
    all_to_all x1, waiting for transfers between devices, on_device(): lax.all_to_all(outgoing, 'wk', 0, 0, tiled=True).reshape(block, -1)  14.2 us
    all_to_all x1, starting transfers between devices, on_device(): lax.all_to_all(outgoing, 'wk', 0, 0, tiled=True).reshape(block, -1)  6.19 us
    all_to_all x1, waiting for transfers between devices, on_device(): returned = lax.all_to_all(product, 'wk', 0, 0, tiled=True)  5.92 us
    ppermute x2, starting transfers between devices, shifted(): lax.ppermute(value, axis, [(i, (i + shift) % size) for i in range(size)])  4.59 us
    all_to_all x1, starting transfers between devices, on_device(): returned = lax.all_to_all(product, 'wk', 0, 0, tiled=True)  4.42 us
    ppermute x2, waiting for transfers between devices, shifted(): lax.ppermute(value, axis, [(i, (i + shift) % size) for i in range(size)])  3.83 us
    dot_general x2, matrix products, on_device(): jnp.dot(right, part, preferred_element_type=jnp.float32)  2.69 us
    dot_general x1, matrix products, on_device(): lax.dot_general(gathered, left, (((0,), (0,)), ((), ())), preferred_eleme...  1.5 us
  transfers between devices with their start and end apart: 4, of which 4 were waited for; matrix products, arithmetic and copies ran while one was open for 4% of the time, Pallas kernels for 0%

profile of v1, /device:TPU:0, one launch (start us, length us, event | category | flops | bytes accessed | tf_op | source)
XLA Modules:
  0.0 62.9 jit_solution(3813704039426773504)
XLA Ops:
  0.0 0.9 %dynamic-slice_bitcast_fusion = bf16[4,32,512]{2,1,0:T(8,128)(2,1)S(1)} fusion(bf16[1,4,32,1024]{3,2,1,0:T(8,128)(2,1)} %param.4, s32[]{:T(128)S(6)} %select_n.83), kind=kLoop, calls=%fused_computation.17 | loop fusion | bytes 262148 | tf_op jit(solution)/shard_map/dynamic_slice | solution.py:18
  0.9 3.0 %collective-permute-start = (bf16[4,32,512]{2,1,0:T(8,128)(2,1)S(1)}, bf16[4,32,512]{2,1,0:T(8,128)(2,1)S(1)}, u32[]{:S(2)}, u32[]{:S(2)}) collective-permute-start(bf16[4,32,512]{2,1,0:T(8,128)(2,1)S(1)} %dynamic-slice_bitcast_fusion), channel_id=1, source_target_pairs={{0,16},{16,0},{1,17},{17,1},{2,18},{18,2},{3,19},{19,3},{4,20},{20... | collective-permute-start | bytes 393224 | tf_op jit(solution)/shard_map/ppermute | solution.py:9
  3.9 0.7 %iota_compare_fusion = pred[16,4]{0,1:T(4,128)(4,1)S(1)} fusion(s32[4]{0:T(128)} %param.6), kind=kLoop, calls=%fused_computation.31 | loop fusion | flops 64 | bytes 80 | tf_op jit(solution)/shard_map/eq | solution.py:51
  4.7 2.8 %collective-permute-done = bf16[4,32,512]{2,1,0:T(8,128)(2,1)S(1)} collective-permute-done((bf16[4,32,512]{2,1,0:T(8,128)(2,1)S(1)}, bf16[4,32,512]{2,1,0:T(8,128)(2,1)S(1)}, u32[]{:S(2)}, u32[]{:S(2)}) %collective-permute-start) | collective-permute-done | bytes 131104 | tf_op jit(solution)/shard_map/ppermute | solution.py:9
  7.4 0.9 %fusion.8 = bf16[4,32,512]{2,1,0:T(8,128)(2,1)S(1)} fusion(bf16[4,32,512]{2,1,0:T(8,128)(2,1)S(1)} %collective-permute-done, bf16[1,4,32,1024]{3,2,1,0:T(8,128)(2,1)} %param.4, s32[]{:T(128)S(6)} %select_n.81), kind=kLoop, calls=%fused_computation.14 | loop fusion | flops 262144 | bytes 393220 | tf_op jit(solution)/shard_map/convert_element_type | solution.py:23
  8.4 0.0 copy-start
  8.4 0.0 copy-start.1
  8.4 1.0 %select_select_fusion = bf16[16,32,512]{2,1,0:T(8,128)(2,1)} fusion(pred[16]{0:T(512)(128)(4,1)S(1)} %get-tuple-element.22, pred[16]{0:T(512)(128)(4,1)S(1)} %get-tuple-element.23, pred[16]{0:T(512)(128)(4,1)S(1)} %get-tuple-element.24, pred[16]{0:T(512)(128)(4,1)S(1)} %get-tuple-element.21, bf16[32,512]{1,0:T(8,128)(2,1)S(1)} %get-tuple-element.12, ...), kind=kLoop, calls=%fused_computation.9 | loop fusion | flops 1048576 | bytes 655424 | tf_op jit(solution)/shard_map/jit(_where)/select_n | solution.py:54
  9.4 6.2 %all-to-all-start = ((bf16[16,32,512]{2,1,0:T(8,128)(2,1)}), bf16[16,32,512]{2,1,0:T(8,128)(2,1)S(1)}, u32[]{:S(2)}, u32[]{:S(2)}) async-start(bf16[16,32,512]{2,1,0:T(8,128)(2,1)} %select_select_fusion), calls=%async_computation | async-start | bytes 1048576 | tf_op jit(solution)/shard_map/all_to_all | solution.py:55
  15.6 14.2 %all-to-all-done = bf16[16,32,512]{2,1,0:T(8,128)(2,1)S(1)} async-done(((bf16[16,32,512]{2,1,0:T(8,128)(2,1)}), bf16[16,32,512]{2,1,0:T(8,128)(2,1)S(1)}, u32[]{:S(2)}, u32[]{:S(2)}) %all-to-all-start) | async-done | bytes 524320 | tf_op jit(solution)/shard_map/all_to_all | solution.py:55
  29.9 1.5 %convolution_convert_fusion = bf16[512,512]{1,0:T(8,128)(2,1)S(1)} fusion(bf16[512,512]{1,0:T(8,128)(2,1)S(1)} %bitcast.65, bf16[1,5,512,512]{3,2,1,0:T(8,128)(2,1)} %param.5), kind=kOutput, calls=%fused_computation | convolution fusion | flops 268697600 | bytes 1572864 | tf_op jit(solution)/shard_map/dot_general | solution.py:59
  31.5 1.6 %collective-permute-start.1 = (bf16[512,256]{1,0:T(8,128)(2,1)S(1)}, bf16[512,256]{1,0:T(8,128)(2,1)S(1)}, u32[]{:S(2)}, u32[]{:S(2)}) collective-permute-start(bf16[512,256]{1,0:T(8,128)(2,1)S(1)} %get-tuple-element.9), channel_id=1, source_target_pairs={{0,16},{16,0},{1,17},{17,1},{2,18},{18,2},{3,19},{19,3},{4,20},{20... | collective-permute-start | bytes 786440 | tf_op jit(solution)/shard_map/ppermute | solution.py:9
  33.0 0.0 copy-done
  33.0 0.6 %fusion.11 = s32[]{:T(128)} fusion(s32[4]{0:T(128)S(1)} %copy-done, s32[]{:T(128)S(6)} %axis_index.26), kind=kLoop, calls=%fused_computation.37 | loop fusion | flops 11 | bytes 24 | tf_op jit(solution)/shard_map/reduce_sum | solution.py:57
  35.6 0.0 copy-done.1
  35.6 0.7 %constant_dynamic-slice_fusion.1 = (s32[1,1]{0,1:T(1,128)}, s32[1,1]{0,1:T(1,128)}) fusion(s32[4,2]{0,1:T(2,128)S(1)} %copy-done.1, s32[]{:T(128)S(6)} %select_n.79), kind=kLoop, calls=%fused_computation.30 | loop fusion | bytes 20 | tf_op jit(solution)/shard_map/dynamic_slice | solution.py:65
  38.8 1.1 %collective-permute-done.1 = bf16[512,256]{1,0:T(8,128)(2,1)S(1)} collective-permute-done((bf16[512,256]{1,0:T(8,128)(2,1)S(1)}, bf16[512,256]{1,0:T(8,128)(2,1)S(1)}, u32[]{:S(2)}, u32[]{:S(2)}) %collective-permute-start.1) | collective-permute-done | bytes 262176 | tf_op jit(solution)/shard_map/ppermute | solution.py:9
  39.9 1.3 %convolution_convert_fusion.2 = bf16[512,256]{1,0:T(8,128)(2,1)S(1)} fusion(bf16[1,5,512,512]{3,2,1,0:T(8,128)(2,1)} %param.5, s32[]{:T(128)S(6)} %select_n.80, bf16[1024,256]{1,0:T(8,128)(2,1)S(1)} %constant_dynamic-update-slice_fusion), kind=kOutput, calls=%fused_computation.2 | convolution fusion | flops 134348800 | bytes 1048580 | tf_op jit(solution)/shard_map/dot_general | solution.py:67
  41.3 1.3 %convolution_convert_fusion.1 = bf16[512,256]{1,0:T(8,128)(2,1)S(1)} fusion(bf16[1,5,512,512]{3,2,1,0:T(8,128)(2,1)} %param.5, s32[]{:T(128)S(6)} %select_n.94, bf16[1024,256]{1,0:T(8,128)(2,1)S(1)} %constant_dynamic-update-slice_fusion), kind=kOutput, calls=%fused_computation.1 | convolution fusion | flops 134348800 | bytes 1048580 | tf_op jit(solution)/shard_map/dot_general | solution.py:67
  42.6 0.8 %pad_maximum_fusion = bf16[1024,256]{1,0:T(8,128)(2,1)} fusion(bf16[512,256]{1,0:T(8,128)(2,1)S(1)} %convolution_convert_fusion.1, bf16[512,256]{1,0:T(8,128)(2,1)S(1)} %convolution_convert_fusion.2), kind=kLoop, calls=%fused_computation.3 | loop fusion | flops 1048576 | bytes 1048576 | tf_op jit(solution)/shard_map/concatenate | solution.py:68
  43.4 4.4 %all-to-all-start.1 = ((bf16[16,64,256]{2,1,0:T(8,128)(2,1)}), bf16[16,64,256]{2,1,0:T(8,128)(2,1)S(1)}, u32[]{:S(2)}, u32[]{:S(2)}) async-start(bf16[16,64,256]{2,1,0:T(8,128)(2,1)} %bitcast.18), calls=%async_computation.1 | async-start | bytes 1048576 | tf_op jit(solution)/shard_map/all_to_all | solution.py:71
  47.9 0.7 %fusion.12 = (s32[1]{0:T(128)}, s32[1]{0:T(128)}, s32[1]{0:T(128)}, s32[1]{0:T(128)}) fusion(s32[4]{0:T(128)S(1)} %copy-done), kind=kLoop, calls=%fused_computation.39 | loop fusion | bytes 32 | tf_op jit(solution)/shard_map/slice | solution.py:74
  56.2 5.9 %all-to-all-done.1 = bf16[16,64,256]{2,1,0:T(8,128)(2,1)S(1)} async-done(((bf16[16,64,256]{2,1,0:T(8,128)(2,1)}), bf16[16,64,256]{2,1,0:T(8,128)(2,1)S(1)}, u32[]{:S(2)}, u32[]{:S(2)}) %all-to-all-start.1) | async-done | bytes 524320 | tf_op jit(solution)/shard_map/all_to_all | solution.py:71
  62.2 0.7 %maximum_convert_fusion = f32[4,256,64]{1,2,0:T(8,128)} fusion(bf16[1,256,64]{1,2,0:T(8,128)(2,1)S(1)} %get-tuple-element.6, bf16[1,256,64]{1,2,0:T(8,128)(2,1)S(1)} %get-tuple-element.7, bf16[1,256,64]{1,2,0:T(8,128)(2,1)S(1)} %get-tuple-element.8, bf16[1,256,64]{1,2,0:T(8,128)(2,1)S(1)} %get-tuple-element.5), kind=kLoop, calls=%fused_computation.16 | loop fusion | flops 262144 | bytes 393216 | tf_op jit(solution)/shard_map/stack | solution.py:76
  (6 shorter events, 0.1 us)
Async XLA Ops:
  0.9 6.5 %collective-permute-start = (bf16[4,32,512]{2,1,0:T(8,128)(2,1)S(1)}, bf16[4,32,512]{2,1,0:T(8,128)(2,1)S(1)}, u32[]{:S(2)}, u32[]{:S(2)}) collective-permute-start(bf16[4,32,512]{2,1,0:T(8,128)(2,1)S(1)} %dynamic-slice_bitcast_fusion), channel_id=1, source_target_pairs={{0,16},{16,0},{1,17},{17,1},{2,18},{18,2},{3,19},{19,3},{4,20},{20... | collective-permute-start | bytes 393224 | tf_op jit(solution)/shard_map/ppermute | solution.py:9
  8.4 24.6 %copy-start = (s32[4]{0:T(128)S(1)}, s32[4]{0:T(128)}, u32[]{:S(2)}) copy-start(s32[4]{0:T(128)} %param.6) | copy-start | bytes 52
  8.4 27.2 %copy-start.1 = (s32[4,2]{0,1:T(2,128)S(1)}, s32[4,2]{0,1:T(2,128)}, u32[]{:S(2)}) copy-start(s32[4,2]{0,1:T(2,128)} %param.7) | copy-start | bytes 100
  9.4 20.5 %all-to-all-start = ((bf16[16,32,512]{2,1,0:T(8,128)(2,1)}), bf16[16,32,512]{2,1,0:T(8,128)(2,1)S(1)}, u32[]{:S(2)}, u32[]{:S(2)}) async-start(bf16[16,32,512]{2,1,0:T(8,128)(2,1)} %select_select_fusion), calls=%async_computation | async-start | bytes 1048576 | tf_op jit(solution)/shard_map/all_to_all | solution.py:55
  31.5 8.4 %collective-permute-start.1 = (bf16[512,256]{1,0:T(8,128)(2,1)S(1)}, bf16[512,256]{1,0:T(8,128)(2,1)S(1)}, u32[]{:S(2)}, u32[]{:S(2)}) collective-permute-start(bf16[512,256]{1,0:T(8,128)(2,1)S(1)} %get-tuple-element.9), channel_id=1, source_target_pairs={{0,16},{16,0},{1,17},{17,1},{2,18},{18,2},{3,19},{19,3},{4,20},{20... | collective-permute-start | bytes 786440 | tf_op jit(solution)/shard_map/ppermute | solution.py:9
  43.4 18.7 %all-to-all-start.1 = ((bf16[16,64,256]{2,1,0:T(8,128)(2,1)}), bf16[16,64,256]{2,1,0:T(8,128)(2,1)S(1)}, u32[]{:S(2)}, u32[]{:S(2)}) async-start(bf16[16,64,256]{2,1,0:T(8,128)(2,1)} %bitcast.18), calls=%async_computation.1 | async-start | bytes 1048576 | tf_op jit(solution)/shard_map/all_to_all | solution.py:71

commit v2 on v0

v2 whole, which is shorter than its diff:
```python
import jax
import jax.numpy as jnp
from jax import lax
from jax.sharding import PartitionSpec as P


def shifted(value, axis, shift):
    size = lax.axis_size(axis)
    return lax.ppermute(value, axis, [(i, (i + shift) % size) for i in range(size)])


def on_device(grads, bank, owners, col_map):
    layers, _, total_width = grads.shape[1:]
    block = bank.shape[2]
    groups, workers = lax.axis_size("grp"), lax.axis_size("wk")
    me, worker = lax.axis_index("grp"), lax.axis_index("wk")
    width = total_width // groups
    share = block // groups

    def columns(group):
        return lax.dynamic_slice_in_dim(grads[0], group * width, width, 2)

    summed = columns(me).astype(jnp.float32)
    for shift in range(1, groups):
        summed += shifted(columns((me + shift) % groups), "grp", shift).astype(jnp.float32)
    summed = summed.astype(jnp.bfloat16)

    serves = owners[None, :] == jnp.arange(workers, dtype=owners.dtype)[:, None]
    outgoing = jnp.broadcast_to(summed[0], (workers,) + summed.shape[1:])
    for layer in range(1, layers):
        outgoing = jnp.where(serves[:, layer, None, None], summed[layer][None], outgoing)
    gathered = lax.all_to_all(outgoing, "wk", 0, 0, tiled=True).reshape(block, width)

    my_layer = jnp.sum(jnp.where(owners == worker, jnp.arange(layers), 0))
    left = bank[0, 0]
    products = [None] * groups
    for shift in reversed(range(groups)):
        rows = lax.dynamic_slice_in_dim(left, (me + shift) % groups * share, share, 0)
        product = jnp.dot(rows, gathered, preferred_element_type=jnp.float32)
        product = product.astype(jnp.bfloat16)
        products[shift] = shifted(product, "grp", shift) if shift else product
    blocks = col_map.shape[1]
    full = jnp.zeros((groups, share, width), jnp.bfloat16)
    for shift in range(groups):
        full = lax.dynamic_update_slice_in_dim(
            full, products[shift][None], (me + groups - shift) % groups, 0
        )
    full = full.transpose(1, 0, 2).reshape(share, blocks, block)
    rights = jnp.stack(
        [
            lax.dynamic_index_in_dim(bank[0], 1 + col_map[my_layer, index], 0, False)
            for index in range(blocks)
        ]
    )
    product = jnp.einsum("jab,rjb->jar", rights, full, preferred_element_type=jnp.float32)
    product = product.astype(jnp.bfloat16)

    product = product.reshape(workers, -1, share)
    returned = lax.all_to_all(product, "wk", 0, 0, tiled=True)
    results = []
    for layer in range(layers):
        part = lax.dynamic_index_in_dim(returned, owners[layer], 0, False)
        results.append(part.astype(jnp.float32).T)
    return jnp.stack(results)


def solution(mesh):
    in_specs = (P("grp", None, "wk", None), P("wk", None, None, None), P(), P())
    out_specs = P(None, "grp", "wk")
    return jax.shard_map(
        on_device, mesh=mesh, in_specs=in_specs, out_specs=out_specs, check_vma=False
    )
```

time: 351 us -> 59.9 us (0.17)
  waiting for transfers between devices: 289 us -> 22.1 us
  local copies, waits for them, and re-layouts: 35.2 us -> 3.81 us
  starting transfers between devices: 0.2 us -> 15.2 us
  between operations: 16.2 us -> 12.4 us
    psum x2 -> x0, waiting for transfers between devices: 168 us -> none  [the longest x1 140 us: spread(): return lax.psum(jnp.where(mine, value, jnp.zeros_like(value)), axis)]
    all_gather x4 -> x0, waiting for transfers between devices: 120 us -> none  [on_device(): lax.all_gather(summed, 'wk', axis=0, tiled=True)]
    gather x8 -> x0, local copies, waits for them, and re-layouts: 13.9 us -> none  [on_device(): chosen = jnp.take(bank[0, 1:], col_map[layer_index], axis=0)]
    all_to_all x0 -> x2, waiting for transfers between devices: none -> 12.8 us  [the longest x1 6.89 us: on_device(): lax.all_to_all(outgoing, 'wk', 0, 0, tiled=True).reshape(block, width)]
    all_to_all x0 -> x2, starting transfers between devices: none -> 10.6 us  [the longest x1 6.19 us: on_device(): lax.all_to_all(outgoing, 'wk', 0, 0, tiled=True).reshape(block, width)]
    ppermute x0 -> x2, waiting for transfers between devices: none -> 9.28 us  [shifted(): lax.ppermute(value, axis, [(i, (i + shift) % size) for i in range(size)])]
    all_gather x4 -> x0, local copies, waits for them, and re-layouts: 6.76 us -> none  [on_device(): lax.all_gather(summed, 'wk', axis=0, tiled=True)]
    unnamed x15 -> x4, local copies, waits for them, and re-layouts: 5.65 us -> 0.01 us
  transfers between devices with their start and end apart: 6 -> 4, of which waited for: 6 -> 4; matrix products, arithmetic and copies ran while one was open for 9% -> 8% of each run, Pallas kernels for 0% -> 0%
where the time goes in v2:
time: 59.9 us; the launch traced here: 59.3 us
  waiting for transfers between devices  22.1 us (37%)
  starting transfers between devices  15.2 us (25%)
  between operations  12.4 us (21%)
  other arithmetic  3.99 us (7%)
  local copies, waits for them, and re-layouts  3.81 us (6%)
  matrix products  1.85 us (3%)
    ppermute x2, waiting for transfers between devices, shifted(): lax.ppermute(value, axis, [(i, (i + shift) % size) for i in range(size)])  9.28 us
    all_to_all x1, waiting for transfers between devices, on_device(): lax.all_to_all(outgoing, 'wk', 0, 0, tiled=True).reshape(block, width)  6.89 us
    all_to_all x1, starting transfers between devices, on_device(): lax.all_to_all(outgoing, 'wk', 0, 0, tiled=True).reshape(block, width)  6.19 us
    all_to_all x1, waiting for transfers between devices, on_device(): returned = lax.all_to_all(product, 'wk', 0, 0, tiled=True)  5.91 us
    ppermute x2, starting transfers between devices, shifted(): lax.ppermute(value, axis, [(i, (i + shift) % size) for i in range(size)])  4.59 us
    all_to_all x1, starting transfers between devices, on_device(): returned = lax.all_to_all(product, 'wk', 0, 0, tiled=True)  4.41 us
    slice x1, local copies, waits for them, and re-layouts, on_device(): left = bank[0, 0]  1.47 us
    dot_general x1, matrix products, on_device(): jnp.einsum('jab,rjb->jar', rights, full, preferred_element_type=jnp.float32)  1.26 us
  transfers between devices with their start and end apart: 4, of which 4 were waited for; matrix products, arithmetic and copies ran while one was open for 8% of the time, Pallas kernels for 0%

profile of v2, /device:TPU:0, one launch (start us, length us, event | category | flops | bytes accessed | tf_op | source)
XLA Modules:
  0.0 59.3 jit_solution(14287089516974435791)
XLA Ops:
  0.0 0.0 copy-start
  0.0 0.0 copy-start.1
  0.0 0.9 %dynamic-slice_bitcast_fusion.2 = bf16[4,32,512]{2,1,0:T(8,128)(2,1)S(1)} fusion(bf16[1,4,32,1024]{3,2,1,0:T(8,128)(2,1)} %param.4, s32[]{:T(128)S(6)} %select_n.83), kind=kLoop, calls=%fused_computation.20 | loop fusion | bytes 262148 | tf_op jit(solution)/shard_map/dynamic_slice | solution.py:21
  0.9 3.0 %collective-permute-start = (bf16[4,32,512]{2,1,0:T(8,128)(2,1)S(1)}, bf16[4,32,512]{2,1,0:T(8,128)(2,1)S(1)}, u32[]{:S(2)}, u32[]{:S(2)}) collective-permute-start(bf16[4,32,512]{2,1,0:T(8,128)(2,1)S(1)} %dynamic-slice_bitcast_fusion.2), channel_id=1, source_target_pairs={{0,16},{16,0},{1,17},{17,1},{2,18},{18,2},{3,19},{19,3},{4,20},{20... | collective-permute-start | bytes 393224 | tf_op jit(solution)/shard_map/ppermute | solution.py:9
  4.0 0.7 %iota_compare_fusion = pred[16,4]{0,1:T(4,128)(4,1)S(1)} fusion(s32[4]{0:T(128)} %param.6), kind=kLoop, calls=%fused_computation.32 | loop fusion | flops 64 | bytes 80 | tf_op jit(solution)/shard_map/eq | solution.py:28
  4.7 2.8 %collective-permute-done = bf16[4,32,512]{2,1,0:T(8,128)(2,1)S(1)} collective-permute-done((bf16[4,32,512]{2,1,0:T(8,128)(2,1)S(1)}, bf16[4,32,512]{2,1,0:T(8,128)(2,1)S(1)}, u32[]{:S(2)}, u32[]{:S(2)}) %collective-permute-start) | collective-permute-done | bytes 131104 | tf_op jit(solution)/shard_map/ppermute | solution.py:9
  7.5 0.9 %fusion.6 = bf16[4,32,512]{2,1,0:T(8,128)(2,1)S(1)} fusion(bf16[4,32,512]{2,1,0:T(8,128)(2,1)S(1)} %collective-permute-done, bf16[1,4,32,1024]{3,2,1,0:T(8,128)(2,1)} %param.4, s32[]{:T(128)S(6)} %select_n.81), kind=kLoop, calls=%fused_computation.13 | loop fusion | flops 262144 | bytes 393220 | tf_op jit(solution)/shard_map/convert_element_type | solution.py:26
  8.4 1.0 %select_select_fusion = bf16[16,32,512]{2,1,0:T(8,128)(2,1)} fusion(pred[16]{0:T(512)(128)(4,1)S(1)} %get-tuple-element.23, pred[16]{0:T(512)(128)(4,1)S(1)} %get-tuple-element.24, pred[16]{0:T(512)(128)(4,1)S(1)} %get-tuple-element.22, bf16[32,512]{1,0:T(8,128)(2,1)S(1)} %get-tuple-element.13, bf16[32,512]{1,0:T(8,128)(2,1)S(1)} %get-tuple-element.14, ...), kind=kLoop, calls=%fused_computation.9 | loop fusion | flops 786432 | bytes 655408 | tf_op jit(solution)/shard_map/jit(_where)/select_n | solution.py:31
  9.4 6.2 %all-to-all-start = ((bf16[16,32,512]{2,1,0:T(8,128)(2,1)}), bf16[16,32,512]{2,1,0:T(8,128)(2,1)S(1)}, u32[]{:S(2)}, u32[]{:S(2)}) async-start(bf16[16,32,512]{2,1,0:T(8,128)(2,1)} %select_select_fusion), calls=%async_computation | async-start | bytes 1048576 | tf_op jit(solution)/shard_map/all_to_all | solution.py:32
  15.6 0.0 copy-done
  15.6 0.6 %fusion.13 = s32[]{:T(128)} fusion(s32[4]{0:T(128)S(1)} %copy-done, s32[]{:T(128)S(6)} %axis_index.22), kind=kLoop, calls=%fused_computation.37 | loop fusion | flops 11 | bytes 24 | tf_op jit(solution)/shard_map/reduce_sum | solution.py:34
  18.2 0.0 copy-done.1
  18.2 0.7 %constant_dynamic-slice_fusion = (s32[1,1]{0,1:T(1,128)}, s32[1,1]{0,1:T(1,128)}) fusion(s32[4,2]{0,1:T(2,128)S(1)} %copy-done.1, s32[]{:T(128)S(6)} %select_n.76), kind=kLoop, calls=%fused_computation.31 | loop fusion | bytes 20 | tf_op jit(solution)/shard_map/dynamic_slice | solution.py:51
  21.5 1.5 %fusion.15 = (bf16[1,1,512,512]{3,2,1,0:T(8,128)(2,1)S(1)}, bf16[1,512,512]{2,1,0:T(8,128)(2,1)S(1)}, bf16[1,512,512]{2,1,0:T(8,128)(2,1)S(1)}) fusion(bf16[1,5,512,512]{3,2,1,0:T(8,128)(2,1)} %param.5, s32[]{:T(128)S(6)} %select_n.77, s32[]{:T(128)S(6)} %select_n.78), kind=kLoop, calls=%fused_computation.40 | loop fusion | bytes 3145736 | tf_op jit(solution)/shard_map/slice | solution.py:35
  23.0 6.9 %all-to-all-done = bf16[16,32,512]{2,1,0:T(8,128)(2,1)S(1)} async-done(((bf16[16,32,512]{2,1,0:T(8,128)(2,1)}), bf16[16,32,512]{2,1,0:T(8,128)(2,1)S(1)}, u32[]{:S(2)}, u32[]{:S(2)}) %all-to-all-start) | async-done | bytes 524320 | tf_op jit(solution)/shard_map/all_to_all | solution.py:32
  29.9 0.3 convolution_convert_fusion.1
  30.2 1.6 %collective-permute-start.1 = (bf16[256,512]{1,0:T(8,128)(2,1)S(1)}, bf16[256,512]{1,0:T(8,128)(2,1)S(1)}, u32[]{:S(2)}, u32[]{:S(2)}) collective-permute-start(bf16[256,512]{1,0:T(8,128)(2,1)S(1)} %convolution_convert_fusion.1), channel_id=1, source_target_pairs={{0,16},{16,0},{1,17},{17,1},{2,18},{18,2},{3,19},{19,3},{4,20},{20... | collective-permute-start | bytes 786440 | tf_op jit(solution)/shard_map/ppermute | solution.py:9
  31.8 0.3 fusion.1
  32.1 6.5 %collective-permute-done.1 = bf16[256,512]{1,0:T(8,128)(2,1)S(1)} collective-permute-done((bf16[256,512]{1,0:T(8,128)(2,1)S(1)}, bf16[256,512]{1,0:T(8,128)(2,1)S(1)}, u32[]{:S(2)}, u32[]{:S(2)}) %collective-permute-start.1) | collective-permute-done | bytes 262176 | tf_op jit(solution)/shard_map/ppermute | solution.py:9
  38.6 1.3 %convolution_convert_fusion = bf16[2,512,256]{2,1,0:T(8,128)(2,1)} fusion(bf16[1,512,512]{2,1,0:T(8,128)(2,1)S(1)} %get-tuple-element.7, bf16[1,512,512]{2,1,0:T(8,128)(2,1)S(1)} %get-tuple-element.6, bf16[2,256,512]{2,1,0:T(8,128)(2,1)S(1)} %bitcast_dynamic-update-slice_fusion), kind=kOutput, calls=%fused_computation | convolution fusion | flops 269221888 | bytes 2097152 | tf_op jit(solution)/shard_map/jab,rjb->jar/dot_general | solution.py:55
  39.9 4.4 %all-to-all-start.1 = ((bf16[16,64,256]{2,1,0:T(8,128)(2,1)}), bf16[16,64,256]{2,1,0:T(8,128)(2,1)S(1)}, u32[]{:S(2)}, u32[]{:S(2)}) async-start(bf16[16,64,256]{2,1,0:T(8,128)(2,1)} %bitcast.21), calls=%async_computation.1 | async-start | bytes 1048576 | tf_op jit(solution)/shard_map/all_to_all | solution.py:59
  44.3 0.7 %fusion.16 = (s32[1]{0:T(128)}, s32[1]{0:T(128)}, s32[1]{0:T(128)}, s32[1]{0:T(128)}) fusion(s32[4]{0:T(128)S(1)} %copy-done), kind=kLoop, calls=%fused_computation.41 | loop fusion | bytes 32 | tf_op jit(solution)/shard_map/slice | solution.py:62
  52.7 5.9 %all-to-all-done.1 = bf16[16,64,256]{2,1,0:T(8,128)(2,1)S(1)} async-done(((bf16[16,64,256]{2,1,0:T(8,128)(2,1)}), bf16[16,64,256]{2,1,0:T(8,128)(2,1)S(1)}, u32[]{:S(2)}, u32[]{:S(2)}) %all-to-all-start.1) | async-done | bytes 524320 | tf_op jit(solution)/shard_map/all_to_all | solution.py:59
  58.6 0.7 %maximum_convert_fusion = f32[4,256,64]{1,2,0:T(8,128)} fusion(bf16[1,256,64]{1,2,0:T(8,128)(2,1)S(1)} %get-tuple-element.9, bf16[1,256,64]{1,2,0:T(8,128)(2,1)S(1)} %get-tuple-element.10, bf16[1,256,64]{1,2,0:T(8,128)(2,1)S(1)} %get-tuple-element.11, bf16[1,256,64]{1,2,0:T(8,128)(2,1)S(1)} %get-tuple-element.8), kind=kLoop, calls=%fused_computation.19 | loop fusion | flops 262144 | bytes 393216 | tf_op jit(solution)/shard_map/stack | solution.py:64
  (5 shorter events, 0.1 us)
Async XLA Ops:
  0.0 15.6 %copy-start = (s32[4]{0:T(128)S(1)}, s32[4]{0:T(128)}, u32[]{:S(2)}) copy-start(s32[4]{0:T(128)} %param.6) | copy-start | bytes 52
  0.0 18.2 %copy-start.1 = (s32[4,2]{0,1:T(2,128)S(1)}, s32[4,2]{0,1:T(2,128)}, u32[]{:S(2)}) copy-start(s32[4,2]{0,1:T(2,128)} %param.7) | copy-start | bytes 100
  0.9 6.5 %collective-permute-start = (bf16[4,32,512]{2,1,0:T(8,128)(2,1)S(1)}, bf16[4,32,512]{2,1,0:T(8,128)(2,1)S(1)}, u32[]{:S(2)}, u32[]{:S(2)}) collective-permute-start(bf16[4,32,512]{2,1,0:T(8,128)(2,1)S(1)} %dynamic-slice_bitcast_fusion.2), channel_id=1, source_target_pairs={{0,16},{16,0},{1,17},{17,1},{2,18},{18,2},{3,19},{19,3},{4,20},{20... | collective-permute-start | bytes 393224 | tf_op jit(solution)/shard_map/ppermute | solution.py:9
  9.4 20.5 %all-to-all-start = ((bf16[16,32,512]{2,1,0:T(8,128)(2,1)}), bf16[16,32,512]{2,1,0:T(8,128)(2,1)S(1)}, u32[]{:S(2)}, u32[]{:S(2)}) async-start(bf16[16,32,512]{2,1,0:T(8,128)(2,1)} %select_select_fusion), calls=%async_computation | async-start | bytes 1048576 | tf_op jit(solution)/shard_map/all_to_all | solution.py:32
  30.2 8.4 %collective-permute-start.1 = (bf16[256,512]{1,0:T(8,128)(2,1)S(1)}, bf16[256,512]{1,0:T(8,128)(2,1)S(1)}, u32[]{:S(2)}, u32[]{:S(2)}) collective-permute-start(bf16[256,512]{1,0:T(8,128)(2,1)S(1)} %convolution_convert_fusion.1), channel_id=1, source_target_pairs={{0,16},{16,0},{1,17},{17,1},{2,18},{18,2},{3,19},{19,3},{4,20},{20... | collective-permute-start | bytes 786440 | tf_op jit(solution)/shard_map/ppermute | solution.py:9
  39.9 18.7 %all-to-all-start.1 = ((bf16[16,64,256]{2,1,0:T(8,128)(2,1)}), bf16[16,64,256]{2,1,0:T(8,128)(2,1)S(1)}, u32[]{:S(2)}, u32[]{:S(2)}) async-start(bf16[16,64,256]{2,1,0:T(8,128)(2,1)} %bitcast.21), calls=%async_computation.1 | async-start | bytes 1048576 | tf_op jit(solution)/shard_map/all_to_all | solution.py:59

commit v3 on v2

v3 whole, which is shorter than its diff:
```python
import jax
import jax.numpy as jnp
from jax import lax
from jax.sharding import PartitionSpec as P


def shifted(value, axis, shift):
    size = lax.axis_size(axis)
    return lax.ppermute(value, axis, [(i, (i + shift) % size) for i in range(size)])


def pick(stack, index):
    return lax.dynamic_index_in_dim(stack, index, 0, False)


def returned_by_parts(gathered, bank, owners, my_columns):
    block = bank.shape[2]
    groups, workers = lax.axis_size("grp"), lax.axis_size("wk")
    me, worker = lax.axis_index("grp"), lax.axis_index("wk")
    size = workers // groups
    part, places = worker // size, owners % size

    share = block // groups
    left, right = lax.optimization_barrier((bank[0, 0], pick(bank[0], 1 + my_columns[me])))
    left_product = jnp.dot(left, gathered, preferred_element_type=jnp.float32)
    left_product = left_product.astype(jnp.bfloat16).reshape(groups, share, block)
    rights = jnp.broadcast_to(right, (groups,) + right.shape)
    product = jnp.einsum("gab,grb->gar", rights, left_product, preferred_element_type=jnp.float32)
    product = product.astype(jnp.bfloat16).reshape(workers, -1, share)

    parts = [
        [group * workers + index * size + place for group in range(groups) for place in range(size)]
        for index in range(groups)
    ]
    arrived = lax.all_to_all(
        product, ("grp", "wk"), 0, 0, axis_index_groups=parts, tiled=True
    ).reshape(groups, size, -1, share)

    def layers_of(index):
        return jnp.stack([pick(pick(arrived, index), place) for place in places])

    result = layers_of(part)
    for shift in range(1, groups):
        other = shifted(layers_of((part + shift) % groups), "wk", shift * size)
        theirs = owners // size == (part + groups - shift) % groups
        result = jnp.where(theirs[:, None, None], other, result)
    return result


def returned_by_rows(gathered, bank, owners, my_columns):
    block = bank.shape[2]
    width = gathered.shape[1]
    groups, workers = lax.axis_size("grp"), lax.axis_size("wk")
    me = lax.axis_index("grp")
    share, blocks = block // groups, my_columns.shape[0]

    full = jnp.zeros((groups, share, width), jnp.bfloat16)
    for shift in reversed(range(groups)):
        rows = lax.dynamic_slice_in_dim(bank[0, 0], (me + shift) % groups * share, share, 0)
        product = jnp.dot(rows, gathered, preferred_element_type=jnp.float32)
        product = product.astype(jnp.bfloat16)
        product = shifted(product, "grp", shift) if shift else product
        source = (me + groups - shift) % groups
        full = lax.dynamic_update_slice_in_dim(full, product[None], source, 0)
    full = full.transpose(1, 0, 2).reshape(share, blocks, block)
    rights = jnp.stack([pick(bank[0], 1 + my_columns[index]) for index in range(blocks)])
    product = jnp.einsum("jab,rjb->jar", rights, full, preferred_element_type=jnp.float32)
    product = product.astype(jnp.bfloat16).reshape(workers, -1, share)
    arrived = lax.all_to_all(product, "wk", 0, 0, tiled=True)
    return jnp.stack([pick(arrived, owner) for owner in owners])


def on_device(grads, bank, owners, col_map):
    layers, _, total_width = grads.shape[1:]
    block = bank.shape[2]
    groups, workers = lax.axis_size("grp"), lax.axis_size("wk")
    me, worker = lax.axis_index("grp"), lax.axis_index("wk")
    width = total_width // groups

    serves = owners[None, :] == jnp.arange(workers, dtype=owners.dtype)[:, None]

    def columns(group):
        return lax.dynamic_slice_in_dim(grads[0], group * width, width, 2)

    def placed(rows):
        placed_rows = jnp.broadcast_to(rows[0], (workers,) + rows.shape[1:])
        for layer in range(1, layers):
            placed_rows = jnp.where(serves[:, layer, None, None], rows[layer][None], placed_rows)
        return placed_rows.astype(jnp.float32)

    summed = placed(columns(me))
    for shift in range(1, groups):
        summed += placed(shifted(columns((me + shift) % groups), "grp", shift))
    outgoing = summed.astype(jnp.bfloat16)
    gathered = lax.all_to_all(outgoing, "wk", 0, 0, tiled=True).reshape(block, width)

    my_layer = jnp.sum(jnp.where(owners == worker, jnp.arange(layers), 0))
    by_parts = width == block and workers % groups == 0
    returned = returned_by_parts if by_parts else returned_by_rows
    result = returned(gathered, bank, owners, pick(col_map, my_layer))
    return result.astype(jnp.float32).transpose(0, 2, 1)


def solution(mesh):
    in_specs = (P("grp", None, "wk", None), P("wk", None, None, None), P(), P())
    out_specs = P(None, "grp", "wk")
    return jax.shard_map(
        on_device, mesh=mesh, in_specs=in_specs, out_specs=out_specs, check_vma=False
    )
```

time: 59.9 us -> 55.4 us (0.925)
  waiting for transfers between devices: 22.1 us -> 19.3 us
  between operations: 12.4 us -> 10.8 us
    all_to_all x1, waiting for transfers between devices: 5.91 us -> 2.34 us  [returned_by_parts(): lax.all_to_all(product, ('grp', 'wk'), 0, 0, axis_index_groups=parts, til...]
    slice x2 -> x0, local copies, waits for them, and re-layouts: 2.12 us -> none  [the longest x1 1.47 us: on_device(): left = bank[0, 0]]
    all_to_all x1, waiting for transfers between devices: 6.89 us -> 8.5 us  [on_device(): lax.all_to_all(outgoing, 'wk', 0, 0, tiled=True).reshape(block, width)]
    squeeze x0 -> x1, local copies, waits for them, and re-layouts: none -> 1.28 us  [pick(): return lax.dynamic_index_in_dim(stack, index, 0, False)]
    ppermute x2, waiting for transfers between devices: 9.28 us -> 8.46 us  [shifted(): lax.ppermute(value, axis, [(i, (i + shift) % size) for i in range(size)])]
    transpose x0 -> x1, other arithmetic: none -> 0.79 us  [on_device(): return result.astype(jnp.float32).transpose(0, 2, 1)]
    broadcast_in_dim x3, local copies, waits for them, and re-layouts: 0.06 us -> 0.85 us  [placed(): jnp.where(serves[:, layer, None, None], rows[layer][None], placed_rows)]
    another operation x1, other arithmetic: 0.73 us -> 0.02 us  [layers_of(): return jnp.stack([pick(pick(arrived, index), place) for place in places])]
  transfers between devices with their start and end apart: 4 -> 4, of which waited for: 4 -> 4; matrix products, arithmetic and copies ran while one was open for 8% -> 9% of each run, Pallas kernels for 0% -> 0%
where the time goes in v3:
time: 55.4 us; the launch traced here: 54.8 us
  waiting for transfers between devices  19.3 us (35%)
  starting transfers between devices  15.2 us (27%)
  between operations  10.8 us (19%)
  local copies, waits for them, and re-layouts  4.33 us (8%)
  other arithmetic  3.4 us (6%)
  matrix products  1.71 us (3%)
    all_to_all x1, waiting for transfers between devices, on_device(): lax.all_to_all(outgoing, 'wk', 0, 0, tiled=True).reshape(block, width)  8.5 us
    ppermute x2, waiting for transfers between devices, shifted(): lax.ppermute(value, axis, [(i, (i + shift) % size) for i in range(size)])  8.46 us
    all_to_all x1, starting transfers between devices, on_device(): lax.all_to_all(outgoing, 'wk', 0, 0, tiled=True).reshape(block, width)  6.19 us
    ppermute x2, starting transfers between devices, shifted(): lax.ppermute(value, axis, [(i, (i + shift) % size) for i in range(size)])  4.9 us
    all_to_all x1, starting transfers between devices, returned_by_parts(): lax.all_to_all(product, ('grp', 'wk'), 0, 0, axis_index_groups=parts, til...  4.16 us
    all_to_all x1, waiting for transfers between devices, returned_by_parts(): lax.all_to_all(product, ('grp', 'wk'), 0, 0, axis_index_groups=parts, til...  2.34 us
    dot_general x1, matrix products, returned_by_parts(): jnp.einsum('gab,grb->gar', rights, left_product, preferred_element_type=j...  1.28 us
    squeeze x1, local copies, waits for them, and re-layouts, pick(): return lax.dynamic_index_in_dim(stack, index, 0, False)  1.28 us
  transfers between devices with their start and end apart: 4, of which 4 were waited for; matrix products, arithmetic and copies ran while one was open for 9% of the time, Pallas kernels for 0%

profile of v3, /device:TPU:0, one launch (start us, length us, event | category | flops | bytes accessed | tf_op | source)
XLA Modules:
  0.0 54.8 jit_solution(3347837875300658262)
XLA Ops:
  0.0 0.0 copy-start
  0.0 0.0 copy-start.1
  0.0 0.9 %dynamic-slice_bitcast_fusion.1 = bf16[4,32,512]{2,1,0:T(8,128)(2,1)S(1)} fusion(bf16[1,4,32,1024]{3,2,1,0:T(8,128)(2,1)} %param.4, s32[]{:T(128)S(6)} %select_n.132), kind=kLoop, calls=%fused_computation.9 | loop fusion | bytes 262148 | tf_op jit(solution)/shard_map/dynamic_slice | solution.py:83
  0.9 3.0 %collective-permute-start = (bf16[4,32,512]{2,1,0:T(8,128)(2,1)S(1)}, bf16[4,32,512]{2,1,0:T(8,128)(2,1)S(1)}, u32[]{:S(2)}, u32[]{:S(2)}) collective-permute-start(bf16[4,32,512]{2,1,0:T(8,128)(2,1)S(1)} %dynamic-slice_bitcast_fusion.1), channel_id=1, source_target_pairs={{0,16},{16,0},{1,17},{17,1},{2,18},{18,2},{3,19},{19,3},{4,20},{20... | collective-permute-start | bytes 393224 | tf_op jit(solution)/shard_map/ppermute | solution.py:9
  4.0 0.7 %iota_compare_fusion = pred[16,4]{0,1:T(4,128)(4,1)S(1)} fusion(s32[4]{0:T(128)} %param.6), kind=kLoop, calls=%fused_computation.26 | loop fusion | flops 64 | bytes 80 | tf_op jit(solution)/shard_map/eq | solution.py:80
  4.7 0.8 %dynamic-slice_bitcast_fusion.5 = (bf16[32,512]{1,0:T(8,128)(2,1)S(1)}, bf16[32,512]{1,0:T(8,128)(2,1)S(1)}, bf16[32,512]{1,0:T(8,128)(2,1)S(1)}, bf16[32,512]{1,0:T(8,128)(2,1)S(1)}) fusion(bf16[1,4,32,1024]{3,2,1,0:T(8,128)(2,1)} %param.4, s32[]{:T(128)S(6)} %add.138, s32[]{:T(128)S(6)} %select_n.127, s32[]{:T(128)S(6)} %add.140, s32[]{:T(128)S(6)} %add.139), kind=kLoop, calls=%fused_computation.17 | loop fusion | bytes 262160 | tf_op jit(solution)/shard_map/jit(_where)/broadcast_in_dim | solution.py:88
  5.6 1.9 %collective-permute-done = bf16[4,32,512]{2,1,0:T(8,128)(2,1)S(1)} collective-permute-done((bf16[4,32,512]{2,1,0:T(8,128)(2,1)S(1)}, bf16[4,32,512]{2,1,0:T(8,128)(2,1)S(1)}, u32[]{:S(2)}, u32[]{:S(2)}) %collective-permute-start) | collective-permute-done | bytes 131104 | tf_op jit(solution)/shard_map/ppermute | solution.py:9
  7.5 1.2 %add_convert_fusion = bf16[16,32,512]{2,1,0:T(8,128)(2,1)} fusion(pred[16]{0:T(512)(128)(4,1)S(1)} %get-tuple-element.34, pred[16]{0:T(512)(128)(4,1)S(1)} %get-tuple-element.35, pred[16]{0:T(512)(128)(4,1)S(1)} %get-tuple-element.33, bf16[32,512]{1,0:T(8,128)(2,1)S(1)} %get-tuple-element.24, bf16[32,512]{1,0:T(8,128)(2,1)S(1)} %get-tuple-element.25, ...), kind=kLoop, calls=%fused_computation.2 | loop fusion | flops 2621440 | bytes 786480 | tf_op jit(solution)/shard_map/convert_element_type | solution.py:94
  8.7 6.2 %all-to-all-start = ((bf16[16,32,512]{2,1,0:T(8,128)(2,1)}), bf16[16,32,512]{2,1,0:T(8,128)(2,1)S(1)}, u32[]{:S(2)}, u32[]{:S(2)}) async-start(bf16[16,32,512]{2,1,0:T(8,128)(2,1)} %add_convert_fusion), calls=%async_computation | async-start | bytes 1048576 | tf_op jit(solution)/shard_map/all_to_all | solution.py:95
  14.9 0.0 copy-done
  14.9 0.6 %and_select_fusion = (s32[4]{0:T(128)S(1)}, s32[]{:T(128)}) fusion(s32[4]{0:T(128)S(1)} %copy-done, s32[]{:T(128)S(6)} %axis_index.14), kind=kLoop, calls=%fused_computation.27 | loop fusion | flops 55 | bytes 40 | tf_op jit(solution)/shard_map/jit(remainder)/select_n | solution.py:21
  17.5 0.0 copy-done.1
  17.5 0.6 %dynamic_slice.67 = s32[1,1]{0,1:T(1,128)} dynamic-slice(s32[4,2]{0,1:T(2,128)S(1)} %copy-done.1, s32[]{:T(128)S(6)} %select_n.123, s32[]{:T(128)S(6)} %select_n.125), dynamic_slice_sizes={1,1} | dynamic-slice | bytes 12 | tf_op jit(solution)/shard_map/dynamic_slice | solution.py:24
  19.4 1.3 %dynamic-slice_bitcast_fusion = (bf16[512,512]{1,0:T(8,128)(2,1)S(1)}, bf16[512,512]{1,0:T(8,128)(2,1)S(1)}) fusion(bf16[1,5,512,512]{3,2,1,0:T(8,128)(2,1)} %param.5, s32[]{:T(128)S(6)} %select_n.126), kind=kLoop, calls=%fused_computation.4 | loop fusion | bytes 2097156 | tf_op jit(solution)/shard_map/jit(dynamic_index_in_dim)/squeeze | solution.py:13
  20.7 8.5 %all-to-all-done = bf16[16,32,512]{2,1,0:T(8,128)(2,1)S(1)} async-done(((bf16[16,32,512]{2,1,0:T(8,128)(2,1)}), bf16[16,32,512]{2,1,0:T(8,128)(2,1)S(1)}, u32[]{:S(2)}, u32[]{:S(2)}) %all-to-all-start) | async-done | bytes 524320 | tf_op jit(solution)/shard_map/all_to_all | solution.py:95
  29.2 0.4 convolution_convert_fusion
  29.6 1.3 %convolution_convert_fusion.1 = bf16[2,512,256]{2,1,0:T(8,128)(2,1)} fusion(bf16[2,256,512]{2,1,0:T(8,128)(2,1)S(1)} %bitcast.61, bf16[512,512]{1,0:T(8,128)(2,1)S(1)} %get-tuple-element.7), kind=kOutput, calls=%fused_computation.1 | convolution fusion | flops 268697600 | bytes 1572864 | tf_op jit(solution)/shard_map/gab,grb->gar/dot_general | solution.py:28
  30.9 4.2 %all-to-all-start.1 = ((bf16[16,64,256]{2,1,0:T(8,128)(2,1)}), bf16[16,64,256]{2,1,0:T(8,128)(2,1)S(1)}, u32[]{:S(2)}, u32[]{:S(2)}) async-start(bf16[16,64,256]{2,1,0:T(8,128)(2,1)} %bitcast.18), calls=%async_computation.1 | async-start | bytes 1048576 | tf_op jit(solution)/shard_map/all_to_all | solution.py:35
  35.1 0.7 %fusion.3 = (s32[1]{0:T(128)}, s32[1]{0:T(128)}, s32[1]{0:T(128)}, s32[1]{0:T(128)}) fusion(s32[4]{0:T(128)S(1)} %get-tuple-element.31), kind=kLoop, calls=%fused_computation.38 | loop fusion | bytes 32 | tf_op jit(solution)/shard_map/unstack | solution.py:40
  43.2 2.3 %all-to-all-done.1 = bf16[16,64,256]{2,1,0:T(8,128)(2,1)S(1)} async-done(((bf16[16,64,256]{2,1,0:T(8,128)(2,1)}), bf16[16,64,256]{2,1,0:T(8,128)(2,1)S(1)}, u32[]{:S(2)}, u32[]{:S(2)}) %all-to-all-start.1) | async-done | bytes 524320 | tf_op jit(solution)/shard_map/all_to_all | solution.py:35
  45.6 1.9 %collective-permute-start.1 = (bf16[4,64,256]{2,1,0:T(8,128)(2,1)S(1)}, bf16[4,64,256]{2,1,0:T(8,128)(2,1)S(1)}, u32[]{:S(2)}, u32[]{:S(2)}) collective-permute-start(bf16[4,64,256]{2,1,0:T(8,128)(2,1)S(1)} %pad_maximum_fusion), channel_id=1, source_target_pairs={{0,8},{1,9},{2,10},{3,11},{4,12},{5,13},{6,14},{7,15},{8,0},{9,1},... | collective-permute-start | bytes 393224 | tf_op jit(solution)/shard_map/ppermute | solution.py:9
  47.5 6.5 %collective-permute-done.1 = bf16[4,64,256]{2,1,0:T(8,128)(2,1)S(1)} collective-permute-done((bf16[4,64,256]{2,1,0:T(8,128)(2,1)S(1)}, bf16[4,64,256]{2,1,0:T(8,128)(2,1)S(1)}, u32[]{:S(2)}, u32[]{:S(2)}) %collective-permute-start.1) | collective-permute-done | bytes 131104 | tf_op jit(solution)/shard_map/ppermute | solution.py:9
  54.0 0.8 %convert_bitcast_fusion = f32[4,256,64]{1,2,0:T(8,128)} fusion(bf16[4,64,256]{2,1,0:T(8,128)(2,1)S(1)} %collective-permute-done.1, bf16[1,64,256]{2,1,0:T(8,128)(2,1)S(1)} %get-tuple-element.12, bf16[1,64,256]{2,1,0:T(8,128)(2,1)S(1)} %get-tuple-element.13, bf16[1,64,256]{2,1,0:T(8,128)(2,1)S(1)} %get-tuple-element.14, ...), kind=kLoop, calls=%fused_computation.6 | loop fusion | flops 327680 | bytes 524292 | tf_op jit(solution)/shard_map/transpose | solution.py:101
  (5 shorter events, 0.1 us)
Async XLA Ops:
  0.0 14.9 %copy-start = (s32[4]{0:T(128)S(1)}, s32[4]{0:T(128)}, u32[]{:S(2)}) copy-start(s32[4]{0:T(128)} %param.6) | copy-start | bytes 52
  0.0 17.5 %copy-start.1 = (s32[4,2]{0,1:T(2,128)S(1)}, s32[4,2]{0,1:T(2,128)}, u32[]{:S(2)}) copy-start(s32[4,2]{0,1:T(2,128)} %param.7) | copy-start | bytes 100
  0.9 6.5 %collective-permute-start = (bf16[4,32,512]{2,1,0:T(8,128)(2,1)S(1)}, bf16[4,32,512]{2,1,0:T(8,128)(2,1)S(1)}, u32[]{:S(2)}, u32[]{:S(2)}) collective-permute-start(bf16[4,32,512]{2,1,0:T(8,128)(2,1)S(1)} %dynamic-slice_bitcast_fusion.1), channel_id=1, source_target_pairs={{0,16},{16,0},{1,17},{17,1},{2,18},{18,2},{3,19},{19,3},{4,20},{20... | collective-permute-start | bytes 393224 | tf_op jit(solution)/shard_map/ppermute | solution.py:9
  8.7 20.5 %all-to-all-start = ((bf16[16,32,512]{2,1,0:T(8,128)(2,1)}), bf16[16,32,512]{2,1,0:T(8,128)(2,1)S(1)}, u32[]{:S(2)}, u32[]{:S(2)}) async-start(bf16[16,32,512]{2,1,0:T(8,128)(2,1)} %add_convert_fusion), calls=%async_computation | async-start | bytes 1048576 | tf_op jit(solution)/shard_map/all_to_all | solution.py:95
  30.9 14.7 %all-to-all-start.1 = ((bf16[16,64,256]{2,1,0:T(8,128)(2,1)}), bf16[16,64,256]{2,1,0:T(8,128)(2,1)S(1)}, u32[]{:S(2)}, u32[]{:S(2)}) async-start(bf16[16,64,256]{2,1,0:T(8,128)(2,1)} %bitcast.18), calls=%async_computation.1 | async-start | bytes 1048576 | tf_op jit(solution)/shard_map/all_to_all | solution.py:35
  45.6 8.4 %collective-permute-start.1 = (bf16[4,64,256]{2,1,0:T(8,128)(2,1)S(1)}, bf16[4,64,256]{2,1,0:T(8,128)(2,1)S(1)}, u32[]{:S(2)}, u32[]{:S(2)}) collective-permute-start(bf16[4,64,256]{2,1,0:T(8,128)(2,1)S(1)} %pad_maximum_fusion), channel_id=1, source_target_pairs={{0,8},{1,9},{2,10},{3,11},{4,12},{5,13},{6,14},{7,15},{8,0},{9,1},... | collective-permute-start | bytes 393224 | tf_op jit(solution)/shard_map/ppermute | solution.py:9

commit v4 on v3

v4 whole, which is shorter than its diff:
```python
import jax
import jax.numpy as jnp
import numpy as np
from jax import lax
from jax.sharding import PartitionSpec as P

MEMBER_ORDERS = {
    8: (3, 6, 1, 5, 2, 0, 7, 4),
    16: (11, 6, 13, 9, 10, 5, 8, 0, 15, 2, 12, 4, 3, 14, 1, 7),
}


def member_order(size):
    return np.array(MEMBER_ORDERS.get(size, range(size)), np.int32)


def shifted(value, axis, shift):
    size = lax.axis_size(axis)
    return lax.ppermute(value, axis, [(i, (i + shift) % size) for i in range(size)])


def pick(stack, index):
    return lax.dynamic_index_in_dim(stack, index, 0, False)


def scalars_of(values, limit):
    count = values.shape[0]
    if limit**count > 2**31:
        return [values[index] for index in range(count)]
    packed = jnp.sum(values * np.array([limit**index for index in range(count)], np.int32))
    return [packed // limit**index % limit for index in range(count)]


def looked_up(index, table):
    value = jnp.asarray(table[0], jnp.int32)
    for at in range(1, len(table)):
        value = jnp.where(index == at, table[at], value)
    return value


def in_order(rows, order):
    pieces = rows.reshape(len(order), -1, rows.shape[-1])
    return jnp.take(pieces, order, axis=0).reshape(rows.shape)


def transposed_dot(left, right):
    return lax.dot_general(
        left, right, (((0,), (0,)), ((), ())), preferred_element_type=jnp.float32
    ).astype(jnp.bfloat16)


def returned_by_parts(gathered, left, bank, owners, my_columns):
    block = bank.shape[2]
    groups, workers = lax.axis_size("grp"), lax.axis_size("wk")
    me, worker = lax.axis_index("grp"), lax.axis_index("wk")
    size = workers // groups
    share = block // groups
    order = member_order(size)
    part = worker // size
    places = [looked_up(owner % size, np.argsort(order).tolist()) for owner in owners]

    right = in_order(pick(bank[0], 1 + jnp.sum(jnp.where(jnp.arange(groups) == me, my_columns, 0))), order)
    left, right = lax.optimization_barrier((left, right))
    left_product = transposed_dot(gathered, left)
    product = [
        jnp.dot(
            right,
            left_product[:, group * share : (group + 1) * share],
            preferred_element_type=jnp.float32,
        ).astype(jnp.bfloat16)
        for group in range(groups)
    ]
    product = jnp.stack(product).reshape(workers, -1, share)

    parts = [
        [group * workers + index * size + int(place) for group in range(groups) for place in order]
        for index in range(groups)
    ]
    arrived = lax.all_to_all(
        product, ("grp", "wk"), 0, 0, axis_index_groups=parts, tiled=True
    ).reshape(groups, size, -1, share)

    def layers_of(index):
        return jnp.stack([pick(pick(arrived, index), place) for place in places])

    result = layers_of(part)
    for shift in range(1, groups):
        other = shifted(layers_of((part + shift) % groups), "wk", shift * size)
        source = (part + groups - shift) % groups
        theirs = jnp.stack([owner // size == source for owner in owners])
        result = jnp.where(theirs[:, None, None], other, result)
    return result


def returned_by_rows(gathered, left, bank, owners, my_columns):
    block = bank.shape[2]
    width = gathered.shape[1]
    groups, workers = lax.axis_size("grp"), lax.axis_size("wk")
    me = lax.axis_index("grp")
    share, blocks = block // groups, my_columns.shape[0]

    full = jnp.zeros((groups, share, width), jnp.bfloat16)
    for shift in reversed(range(groups)):
        rows = lax.dynamic_slice_in_dim(left, (me + shift) % groups * share, share, 1)
        product = transposed_dot(rows, gathered)
        product = shifted(product, "grp", shift) if shift else product
        source = (me + groups - shift) % groups
        full = lax.dynamic_update_slice_in_dim(full, product[None], source, 0)
    full = full.transpose(1, 0, 2).reshape(share, blocks, block)
    rights = jnp.stack([pick(bank[0], 1 + my_columns[index]) for index in range(blocks)])
    product = jnp.einsum("jab,rjb->jar", rights, full, preferred_element_type=jnp.float32)
    product = product.astype(jnp.bfloat16).reshape(workers, -1, share)
    arrived = lax.all_to_all(product, "wk", 0, 0, tiled=True)
    return jnp.stack([pick(arrived, owner) for owner in owners])


def on_device(grads, bank, owners, col_map):
    layers, _, total_width = grads.shape[1:]
    block = bank.shape[2]
    groups, workers = lax.axis_size("grp"), lax.axis_size("wk")
    me, worker = lax.axis_index("grp"), lax.axis_index("wk")
    width = total_width // groups
    order = member_order(workers)

    serves = owners[None, :] == order[:, None]

    def columns(group):
        return lax.dynamic_slice_in_dim(grads[0], group * width, width, 2)

    def placed(rows):
        placed_rows = jnp.broadcast_to(rows[0], (workers,) + rows.shape[1:])
        for layer in range(1, layers):
            placed_rows = jnp.where(serves[:, layer, None, None], rows[layer][None], placed_rows)
        return placed_rows.astype(jnp.float32)

    summed = placed(columns(me))
    for shift in range(1, groups):
        summed += placed(shifted(columns((me + shift) % groups), "grp", shift))
    outgoing = summed.astype(jnp.bfloat16)
    planes = [[group * workers + int(member) for member in order] for group in range(groups)]
    gathered = lax.all_to_all(
        outgoing, ("grp", "wk"), 0, 0, axis_index_groups=planes, tiled=True
    ).reshape(block, width)

    my_columns = jnp.sum(jnp.where((owners == worker)[:, None], col_map, 0), axis=0)
    owners = scalars_of(owners, workers)
    left = in_order(bank[0, 0], order)
    by_parts = width == block and workers % groups == 0
    returned = returned_by_parts if by_parts else returned_by_rows
    result = returned(gathered, left, bank, owners, my_columns)
    return result.astype(jnp.float32).transpose(0, 2, 1)


def solution(mesh):
    in_specs = (P("grp", None, "wk", None), P("wk", None, None, None), P(), P())
    out_specs = P(None, "grp", "wk")
    return jax.shard_map(
        on_device, mesh=mesh, in_specs=in_specs, out_specs=out_specs, check_vma=False
    )
```

time: 55.4 us -> 52.3 us (0.944)
  between operations: 10.8 us -> 4.4 us
  starting transfers between devices: 15.2 us -> 18.5 us
  other arithmetic: 3.4 us -> 5.07 us
  waiting for transfers between devices: 19.3 us -> 18.5 us
  matrix products: 1.71 us -> 1.07 us
    all_to_all x1, waiting for transfers between devices: 8.5 us -> 5.69 us  [on_device(): lax.all_to_all(outgoing, ('grp', 'wk'), 0, 0, axis_index_groups=planes, t...]
    all_to_all x1, starting transfers between devices: 4.16 us -> 6.31 us  [returned_by_parts(): lax.all_to_all(product, ('grp', 'wk'), 0, 0, axis_index_groups=parts, til...]
    all_to_all x1, waiting for transfers between devices: 2.34 us -> 4.07 us  [returned_by_parts(): lax.all_to_all(product, ('grp', 'wk'), 0, 0, axis_index_groups=parts, til...]
    reduce_sum x0 -> x3, other arithmetic: none -> 1.39 us  [the longest x1 0.64 us: returned_by_parts(): jnp.sum(jnp.where(jnp.arange(groups) == me, my_columns, 0))]
    dynamic_slice x1 -> x2, local copies, waits for them, and re-layouts: 0.02 us -> 1.3 us  [pick(): return lax.dynamic_index_in_dim(stack, index, 0, False)]
    squeeze x1 -> x0, local copies, waits for them, and re-layouts: 1.28 us -> none  [pick(): return lax.dynamic_index_in_dim(stack, index, 0, False)]
    gather x0 -> x2, local copies, waits for them, and re-layouts: none -> 1.16 us  [in_order(): return jnp.take(pieces, order, axis=0).reshape(rows.shape)]
    another operation x0 -> x2, other arithmetic: none -> 0.92 us  [the longest x1 0.84 us: returned_by_parts(): product = jnp.stack(product).reshape(workers, -1, share)]
  transfers between devices with their start and end apart: 4 -> 4, of which waited for: 4 -> 4; matrix products, arithmetic and copies ran while one was open for 9% -> 11% of each run, Pallas kernels for 0% -> 0%
where the time goes in v4:
time: 52.3 us; the launch traced here: 51.8 us
  starting transfers between devices  18.5 us (35%)
  waiting for transfers between devices  18.5 us (35%)
  other arithmetic  5.07 us (10%)
  between operations  4.4 us (8%)
  local copies, waits for them, and re-layouts  4.28 us (8%)
  matrix products  1.07 us (2%)
    ppermute x2, waiting for transfers between devices, shifted(): lax.ppermute(value, axis, [(i, (i + shift) % size) for i in range(size)])  8.7 us
    all_to_all x1, starting transfers between devices, on_device(): lax.all_to_all(outgoing, ('grp', 'wk'), 0, 0, axis_index_groups=planes, t...  6.38 us
    all_to_all x1, starting transfers between devices, returned_by_parts(): lax.all_to_all(product, ('grp', 'wk'), 0, 0, axis_index_groups=parts, til...  6.31 us
    ppermute x2, starting transfers between devices, shifted(): lax.ppermute(value, axis, [(i, (i + shift) % size) for i in range(size)])  5.81 us
    all_to_all x1, waiting for transfers between devices, on_device(): lax.all_to_all(outgoing, ('grp', 'wk'), 0, 0, axis_index_groups=planes, t...  5.69 us
    all_to_all x1, waiting for transfers between devices, returned_by_parts(): lax.all_to_all(product, ('grp', 'wk'), 0, 0, axis_index_groups=parts, til...  4.07 us
    dynamic_slice x2, local copies, waits for them, and re-layouts, pick(): return lax.dynamic_index_in_dim(stack, index, 0, False)  1.3 us
    convert_element_type x1, other arithmetic, on_device(): outgoing = summed.astype(jnp.bfloat16)  1.2 us
  transfers between devices with their start and end apart: 4, of which 4 were waited for; matrix products, arithmetic and copies ran while one was open for 11% of the time, Pallas kernels for 0%

profile of v4, /device:TPU:0, one launch (start us, length us, event | category | flops | bytes accessed | tf_op | source)
XLA Modules:
  0.0 51.8 jit_solution(4563467968644990624)
XLA Ops:
  0.0 0.0 copy-start.2
  0.0 0.0 copy-start.3
  0.0 1.0 %dynamic-slice_bitcast_fusion = bf16[4,32,512]{2,1,0:T(8,128)(2,1)S(1)} fusion(bf16[1,4,32,1024]{3,2,1,0:T(8,128)(2,1)} %param.8, s32[]{:T(128)S(6)} %select_n.276), kind=kLoop, calls=%fused_computation.14 | loop fusion | bytes 262148 | tf_op jit(solution)/shard_map/dynamic_slice | solution.py:128
  1.0 3.0 %collective-permute-start = (bf16[4,32,512]{2,1,0:T(8,128)(2,1)S(1)}, bf16[4,32,512]{2,1,0:T(8,128)(2,1)S(1)}, u32[]{:S(2)}, u32[]{:S(2)}) collective-permute-start(bf16[4,32,512]{2,1,0:T(8,128)(2,1)S(1)} %dynamic-slice_bitcast_fusion), channel_id=1, source_target_pairs={{0,16},{16,0},{1,17},{17,1},{2,18},{18,2},{3,19},{19,3},{4,20},{20... | collective-permute-start | bytes 393224 | tf_op jit(solution)/shard_map/ppermute | solution.py:19
  4.0 0.7 %broadcast_compare_fusion = pred[16,4]{0,1:T(4,128)(4,1)S(1)} fusion(s32[16]{0:T(128)} %constant.428, s32[4]{0:T(128)} %param.10), kind=kLoop, calls=%fused_computation.39 | loop fusion | flops 64 | bytes 144 | tf_op jit(solution)/shard_map/eq | solution.py:125
  4.8 0.8 %dynamic-slice_bitcast_fusion.4 = (bf16[32,512]{1,0:T(8,128)(2,1)S(1)}, bf16[32,512]{1,0:T(8,128)(2,1)S(1)}, bf16[32,512]{1,0:T(8,128)(2,1)S(1)}, bf16[32,512]{1,0:T(8,128)(2,1)S(1)}) fusion(bf16[1,4,32,1024]{3,2,1,0:T(8,128)(2,1)} %param.8, s32[]{:T(128)S(6)} %add.154, s32[]{:T(128)S(6)} %select_n.271, s32[]{:T(128)S(6)} %add.156, s32[]{:T(128)S(6)} %add.155), kind=kLoop, calls=%fused_computation.22 | loop fusion | bytes 262160 | tf_op jit(solution)/shard_map/jit(_where)/broadcast_in_dim | solution.py:133
  5.6 0.0 copy-start.1
  5.6 1.9 %collective-permute-done = bf16[4,32,512]{2,1,0:T(8,128)(2,1)S(1)} collective-permute-done((bf16[4,32,512]{2,1,0:T(8,128)(2,1)S(1)}, bf16[4,32,512]{2,1,0:T(8,128)(2,1)S(1)}, u32[]{:S(2)}, u32[]{:S(2)}) %collective-permute-start) | collective-permute-done | bytes 131104 | tf_op jit(solution)/shard_map/ppermute | solution.py:19
  7.5 1.2 %add_convert_fusion = bf16[16,32,512]{2,1,0:T(8,128)(2,1)} fusion(pred[16]{0:T(512)(128)(4,1)S(1)} %get-tuple-element.28, pred[16]{0:T(512)(128)(4,1)S(1)} %get-tuple-element.29, pred[16]{0:T(512)(128)(4,1)S(1)} %get-tuple-element.27, bf16[32,512]{1,0:T(8,128)(2,1)S(1)} %get-tuple-element.24, bf16[32,512]{1,0:T(8,128)(2,1)S(1)} %get-tuple-element.25, ...), kind=kLoop, calls=%fused_computation.7 | loop fusion | flops 2621440 | bytes 786480 | tf_op jit(solution)/shard_map/convert_element_type | solution.py:139
  8.7 6.4 %all-to-all-start = ((bf16[16,32,512]{2,1,0:T(8,128)(2,1)}), bf16[16,32,512]{2,1,0:T(8,128)(2,1)S(1)}, u32[]{:S(2)}, u32[]{:S(2)}) async-start(bf16[16,32,512]{2,1,0:T(8,128)(2,1)} %add_convert_fusion), calls=%async_computation | async-start | bytes 1048576 | tf_op jit(solution)/shard_map/all_to_all | solution.py:141
  15.1 0.0 copy-done.3
  15.1 0.0 copy-done
  15.1 0.1 select_reduce_fusion
  15.2 0.6 %fusion.4 = s32[]{:T(128)} fusion(s32[2]{0:T(128)S(1)} %select_reduce_fusion, s32[]{:T(128)S(6)} %axis_index.33), kind=kLoop, calls=%fused_computation.41 | loop fusion | flops 5 | bytes 16 | tf_op jit(solution)/shard_map/reduce_sum | solution.py:62
  17.2 0.0 copy-done.2
  17.2 1.3 %constant_dynamic-slice_fusion = (bf16[1,1,512,512]{3,2,1,0:T(8,128)(2,1)S(1)}, bf16[1,1,512,512]{3,2,1,0:T(8,128)(2,1)S(1)}) fusion(bf16[1,5,512,512]{3,2,1,0:T(8,128)(2,1)} %param.9, s32[]{:T(128)S(6)} %select_n.269), kind=kLoop, calls=%fused_computation.33 | loop fusion | bytes 2097156 | tf_op jit(solution)/shard_map/jit(dynamic_index_in_dim)/dynamic_slice | solution.py:23
  18.5 0.6 %gather_fusion = bf16[16,32,512]{2,1,0:T(8,128)(2,1)S(1)} fusion(bf16[16,32,512]{2,1,0:T(8,128)(2,1)S(1)} %bitcast.64, s32[1024]{0:T(1024)S(1)} %pad_clamp_fusion.1), kind=kCustom, calls=%fused_computation | custom fusion | bytes 1048640 | tf_op jit(solution)/shard_map/jit(_take)/gather | solution.py:43
  19.1 0.0 copy-done.1
  19.1 0.6 %gather_fusion.1 = bf16[8,64,512]{2,1,0:T(8,128)(2,1)S(1)} fusion(bf16[8,64,512]{2,1,0:T(8,128)(2,1)S(1)} %bitcast.63, s32[1024]{0:T(1024)S(1)} %pad_clamp_fusion), kind=kCustom, calls=%fused_computation.1 | custom fusion | bytes 1048608 | tf_op jit(solution)/shard_map/jit(_take)/gather | solution.py:43
  19.7 5.7 %all-to-all-done = bf16[16,32,512]{2,1,0:T(8,128)(2,1)S(1)} async-done(((bf16[16,32,512]{2,1,0:T(8,128)(2,1)}), bf16[16,32,512]{2,1,0:T(8,128)(2,1)S(1)}, u32[]{:S(2)}, u32[]{:S(2)}) %all-to-all-start) | async-done | bytes 524320 | tf_op jit(solution)/shard_map/all_to_all | solution.py:141
  25.4 0.5 convolution_convert_fusion
  25.8 0.3 fusion
  26.1 0.3 fusion.1
  26.5 0.8 %pad_maximum_fusion = bf16[2,512,256]{2,1,0:T(8,128)(2,1)} fusion(bf16[1,512,256]{2,1,0:T(8,128)(2,1)S(1)} %fusion.1, bf16[1,512,256]{2,1,0:T(8,128)(2,1)S(1)} %fusion), kind=kLoop, calls=%fused_computation.8 | loop fusion | flops 262144 | bytes 1048576 | tf_op jit(solution)/shard_map/stack | solution.py:73
  27.3 6.3 %all-to-all-start.1 = ((bf16[16,64,256]{2,1,0:T(8,128)(2,1)}), bf16[16,64,256]{2,1,0:T(8,128)(2,1)S(1)}, u32[]{:S(2)}, u32[]{:S(2)}) async-start(bf16[16,64,256]{2,1,0:T(8,128)(2,1)} %bitcast.23), calls=%async_computation.1 | async-start | bytes 1048576 | tf_op jit(solution)/shard_map/all_to_all | solution.py:79
  33.6 0.0 copy-done.4
  33.6 0.6 %multiply_reduce_fusion = s32[]{:T(128)} fusion(s32[4]{0:T(128)S(1)} %copy-done.3, s32[4]{0:T(128)S(1)} %copy-done.4), kind=kLoop, calls=%fused_computation.42 | loop fusion | flops 7 | bytes 36 | tf_op jit(solution)/shard_map/reduce_sum | solution.py:30
  37.2 4.1 %all-to-all-done.1 = bf16[16,64,256]{2,1,0:T(8,128)(2,1)S(1)} async-done(((bf16[16,64,256]{2,1,0:T(8,128)(2,1)}), bf16[16,64,256]{2,1,0:T(8,128)(2,1)S(1)}, u32[]{:S(2)}, u32[]{:S(2)}) %all-to-all-start.1) | async-done | bytes 524320 | tf_op jit(solution)/shard_map/all_to_all | solution.py:79
  41.3 2.8 %collective-permute-start.1 = (bf16[4,64,256]{2,1,0:T(8,128)(2,1)S(1)}, bf16[4,64,256]{2,1,0:T(8,128)(2,1)S(1)}, u32[]{:S(2)}, u32[]{:S(2)}) collective-permute-start(bf16[4,64,256]{2,1,0:T(8,128)(2,1)S(1)} %pad_maximum_fusion.1), channel_id=1, source_target_pairs={{0,8},{1,9},{2,10},{3,11},{4,12},{5,13},{6,14},{7,15},{8,0},{9,1},... | collective-permute-start | bytes 393224 | tf_op jit(solution)/shard_map/ppermute | solution.py:19
  44.1 0.1 pad_add_fusion
  44.2 6.8 %collective-permute-done.1 = bf16[4,64,256]{2,1,0:T(8,128)(2,1)S(1)} collective-permute-done((bf16[4,64,256]{2,1,0:T(8,128)(2,1)S(1)}, bf16[4,64,256]{2,1,0:T(8,128)(2,1)S(1)}, u32[]{:S(2)}, u32[]{:S(2)}) %collective-permute-start.1) | collective-permute-done | bytes 131104 | tf_op jit(solution)/shard_map/ppermute | solution.py:19
  51.0 0.8 %convert_bitcast_fusion = f32[4,256,64]{1,2,0:T(8,128)} fusion(bf16[4,64,256]{2,1,0:T(8,128)(2,1)S(1)} %collective-permute-done.1, bf16[1,64,256]{2,1,0:T(8,128)(2,1)S(1)} %get-tuple-element.12, bf16[1,64,256]{2,1,0:T(8,128)(2,1)S(1)} %get-tuple-element.13, bf16[1,64,256]{2,1,0:T(8,128)(2,1)S(1)} %get-tuple-element.14, ...), kind=kLoop, calls=%fused_computation.11 | loop fusion | flops 327680 | bytes 524292 | tf_op jit(solution)/shard_map/transpose | solution.py:151
  (9 shorter events, 0.1 us)
Async XLA Ops:
  0.0 17.2 %copy-start.2 = (s32[16]{0:T(128)S(1)}, s32[16]{0:T(128)}, u32[]{:S(2)}) copy-start(s32[16]{0:T(128)} %constant.428) | copy-start | bytes 196
  0.0 15.1 %copy-start.3 = (s32[4]{0:T(128)S(1)}, s32[4]{0:T(128)}, u32[]{:S(2)}) copy-start(s32[4]{0:T(128)} %param.10) | copy-start | bytes 52
  0.0 15.1 %copy-start = (s32[4,2]{0,1:T(2,128)S(1)}, s32[4,2]{0,1:T(2,128)}, u32[]{:S(2)}) copy-start(s32[4,2]{0,1:T(2,128)} %param.11) | copy-start | bytes 100
  1.0 6.5 %collective-permute-start = (bf16[4,32,512]{2,1,0:T(8,128)(2,1)S(1)}, bf16[4,32,512]{2,1,0:T(8,128)(2,1)S(1)}, u32[]{:S(2)}, u32[]{:S(2)}) collective-permute-start(bf16[4,32,512]{2,1,0:T(8,128)(2,1)S(1)} %dynamic-slice_bitcast_fusion), channel_id=1, source_target_pairs={{0,16},{16,0},{1,17},{17,1},{2,18},{18,2},{3,19},{19,3},{4,20},{20... | collective-permute-start | bytes 393224 | tf_op jit(solution)/shard_map/ppermute | solution.py:19
  5.6 13.5 %copy-start.1 = (s32[8]{0:T(128)S(1)}, s32[8]{0:T(128)}, u32[]{:S(2)}) copy-start(s32[8]{0:T(128)} %constant.432) | copy-start | bytes 100
  8.7 16.7 %all-to-all-start = ((bf16[16,32,512]{2,1,0:T(8,128)(2,1)}), bf16[16,32,512]{2,1,0:T(8,128)(2,1)S(1)}, u32[]{:S(2)}, u32[]{:S(2)}) async-start(bf16[16,32,512]{2,1,0:T(8,128)(2,1)} %add_convert_fusion), calls=%async_computation | async-start | bytes 1048576 | tf_op jit(solution)/shard_map/all_to_all | solution.py:141
  25.4 8.2 %copy-start.4 = (s32[4]{0:T(128)S(1)}, s32[4]{0:T(128)}, u32[]{:S(2)}) copy-start(s32[4]{0:T(128)} %constant.409.clone) | copy-start | bytes 52
  27.3 14.0 %all-to-all-start.1 = ((bf16[16,64,256]{2,1,0:T(8,128)(2,1)}), bf16[16,64,256]{2,1,0:T(8,128)(2,1)S(1)}, u32[]{:S(2)}, u32[]{:S(2)}) async-start(bf16[16,64,256]{2,1,0:T(8,128)(2,1)} %bitcast.23), calls=%async_computation.1 | async-start | bytes 1048576 | tf_op jit(solution)/shard_map/all_to_all | solution.py:79
  41.3 9.7 %collective-permute-start.1 = (bf16[4,64,256]{2,1,0:T(8,128)(2,1)S(1)}, bf16[4,64,256]{2,1,0:T(8,128)(2,1)S(1)}, u32[]{:S(2)}, u32[]{:S(2)}) collective-permute-start(bf16[4,64,256]{2,1,0:T(8,128)(2,1)S(1)} %pad_maximum_fusion.1), channel_id=1, source_target_pairs={{0,8},{1,9},{2,10},{3,11},{4,12},{5,13},{6,14},{7,15},{8,0},{9,1},... | collective-permute-start | bytes 393224 | tf_op jit(solution)/shard_map/ppermute | solution.py:19

commit v5 on v4

--- a/solution.py
+++ b/solution.py
@@ -2,11 +2,13 @@
 import jax.numpy as jnp
 import numpy as np
 from jax import lax
+from jax.experimental import pallas as pl
+from jax.experimental.pallas import tpu as pltpu
 from jax.sharding import PartitionSpec as P
 
 MEMBER_ORDERS = {
-    8: (3, 6, 1, 5, 2, 0, 7, 4),
-    16: (11, 6, 13, 9, 10, 5, 8, 0, 15, 2, 12, 4, 3, 14, 1, 7),
+    8: (7, 0, 1, 5, 2, 6, 3, 4),
+    16: (11, 7, 13, 2, 6, 10, 5, 8, 12, 15, 9, 4, 3, 14, 1, 0),
 }
 
 
@@ -49,6 +51,37 @@
     ).astype(jnp.bfloat16)
 
 
+def products_kernel(gathered_ref, left_ref, right_ref, product_ref):
+    mixed = lax.dot_general(
+        right_ref[...],
+        gathered_ref[...],
+        (((1,), (1,)), ((), ())),
+        preferred_element_type=jnp.float32,
+    ).astype(jnp.bfloat16)
+    groups, _, share = product_ref.shape
+    for group in range(groups):
+        product_ref[group] = jnp.dot(
+            mixed,
+            left_ref[:, group * share : (group + 1) * share],
+            preferred_element_type=jnp.float32,
+        ).astype(jnp.bfloat16)
+
+
+def products(gathered, left, right, groups):
+    block = left.shape[0]
+    vmem = pl.BlockSpec(memory_space=pltpu.VMEM)
+    return pl.pallas_call(
+        products_kernel,
+        out_shape=jax.ShapeDtypeStruct((groups, block, block // groups), jnp.bfloat16),
+        in_specs=[vmem] * 3,
+        out_specs=vmem,
+        compiler_params=pltpu.CompilerParams(vmem_limit_bytes=8 << 20),
+        cost_estimate=pl.CostEstimate(
+            flops=4 * block**3, bytes_accessed=8 * block**2, transcendentals=0
+        ),
+    )(gathered, left, right)
+
+
 def returned_by_parts(gathered, left, bank, owners, my_columns):
     block = bank.shape[2]
     groups, workers = lax.axis_size("grp"), lax.axis_size("wk")
@@ -59,18 +92,10 @@
     part = worker // size
     places = [looked_up(owner % size, np.argsort(order).tolist()) for owner in owners]
 
-    right = in_order(pick(bank[0], 1 + jnp.sum(jnp.where(jnp.arange(groups) == me, my_columns, 0))), order)
+    column = 1 + jnp.sum(jnp.where(jnp.arange(groups) == me, my_columns, 0))
+    right = in_order(pick(bank[0], column), order)
     left, right = lax.optimization_barrier((left, right))
-    left_product = transposed_dot(gathered, left)
-    product = [
-        jnp.dot(
-            right,
-            left_product[:, group * share : (group + 1) * share],
-            preferred_element_type=jnp.float32,
-        ).astype(jnp.bfloat16)
-        for group in range(groups)
-    ]
-    product = jnp.stack(product).reshape(workers, -1, share)
+    product = products(gathered, left, right, groups).reshape(workers, -1, share)
 
     parts = [
         [group * workers + index * size + int(place) for group in range(groups) for place in order]

time: 52.3 us -> 50.8 us (0.971)
  Pallas kernels: 0 us -> 1.53 us
  starting transfers between devices: 18.5 us -> 17.2 us
  matrix products: 1.07 us -> 0 us
  other arithmetic: 5.07 us -> 4.23 us
    ppermute x2, waiting for transfers between devices: 8.7 us -> 6.99 us  [shifted(): lax.ppermute(value, axis, [(i, (i + shift) % size) for i in range(size)])]
    pallas_call x0 -> x1, Pallas kernels: none -> 1.53 us  [products(): pl.pallas_call(products_kernel, out_shape=jax.ShapeDtypeStruct((groups, b...]
    all_to_all x1, waiting for transfers between devices: 5.69 us -> 7.01 us  [on_device(): lax.all_to_all(outgoing, ('grp', 'wk'), 0, 0, axis_index_groups=planes, t...]
    all_to_all x1, starting transfers between devices: 6.31 us -> 5.08 us  [returned_by_parts(): lax.all_to_all(product, ('grp', 'wk'), 0, 0, axis_index_groups=parts, til...]
    dot_general x3 -> x0, matrix products: 1.07 us -> none  [the longest x2 0.61 us: returned_by_parts(): jnp.dot(right, left_product[:, group * share:(group + 1) * share], prefer...]
    another operation x1 -> x0, other arithmetic: 0.84 us -> none  [returned_by_parts(): product = jnp.stack(product).reshape(workers, -1, share)]
    all_to_all x1, waiting for transfers between devices: 4.07 us -> 4.71 us  [returned_by_parts(): lax.all_to_all(product, ('grp', 'wk'), 0, 0, axis_index_groups=parts, til...]
where the time goes in v5:
time: 50.8 us; the launch traced here: 50.3 us
  waiting for transfers between devices  18.7 us (37%)
  starting transfers between devices  17.2 us (34%)
  between operations  4.38 us (9%)
  local copies, waits for them, and re-layouts  4.28 us (8%)
  other arithmetic  4.23 us (8%)
  Pallas kernels  1.53 us (3%)
    all_to_all x1, waiting for transfers between devices, on_device(): lax.all_to_all(outgoing, ('grp', 'wk'), 0, 0, axis_index_groups=planes, t...  7.01 us
    ppermute x2, waiting for transfers between devices, shifted(): lax.ppermute(value, axis, [(i, (i + shift) % size) for i in range(size)])  6.99 us
    all_to_all x1, starting transfers between devices, on_device(): lax.all_to_all(outgoing, ('grp', 'wk'), 0, 0, axis_index_groups=planes, t...  6.39 us
    ppermute x2, starting transfers between devices, shifted(): lax.ppermute(value, axis, [(i, (i + shift) % size) for i in range(size)])  5.69 us
    all_to_all x1, starting transfers between devices, returned_by_parts(): lax.all_to_all(product, ('grp', 'wk'), 0, 0, axis_index_groups=parts, til...  5.08 us
    all_to_all x1, waiting for transfers between devices, returned_by_parts(): lax.all_to_all(product, ('grp', 'wk'), 0, 0, axis_index_groups=parts, til...  4.71 us
    pallas_call x1, Pallas kernels, products(): pl.pallas_call(products_kernel, out_shape=jax.ShapeDtypeStruct((groups, b...  1.53 us
    dynamic_slice x2, local copies, waits for them, and re-layouts, pick(): return lax.dynamic_index_in_dim(stack, index, 0, False)  1.3 us
  transfers between devices with their start and end apart: 4, of which 4 were waited for; matrix products, arithmetic and copies ran while one was open for 11% of the time, Pallas kernels for 0%

profile of v5, /device:TPU:0, one launch (start us, length us, event | category | flops | bytes accessed | tf_op | source)
XLA Modules:
  0.0 50.3 jit_solution(1920360773892136974)
XLA Ops:
  0.0 0.0 copy-start.2
  0.0 0.0 copy-start.3
  0.0 0.0 copy-start
  0.0 1.0 %dynamic-slice_bitcast_fusion = bf16[4,32,512]{2,1,0:T(8,128)(2,1)S(1)} fusion(bf16[1,4,32,1024]{3,2,1,0:T(8,128)(2,1)} %param.8, s32[]{:T(128)S(6)} %select_n.269), kind=kLoop, calls=%fused_computation.6 | loop fusion | bytes 262148 | tf_op jit(solution)/shard_map/dynamic_slice | solution.py:153
  1.0 3.0 %collective-permute-start = (bf16[4,32,512]{2,1,0:T(8,128)(2,1)S(1)}, bf16[4,32,512]{2,1,0:T(8,128)(2,1)S(1)}, u32[]{:S(2)}, u32[]{:S(2)}) collective-permute-start(bf16[4,32,512]{2,1,0:T(8,128)(2,1)S(1)} %dynamic-slice_bitcast_fusion), channel_id=1, source_target_pairs={{0,16},{16,0},{1,17},{17,1},{2,18},{18,2},{3,19},{19,3},{4,20},{20... | collective-permute-start | bytes 393224 | tf_op jit(solution)/shard_map/ppermute | solution.py:21
  4.0 0.7 %broadcast_compare_fusion = pred[16,4]{0,1:T(4,128)(4,1)S(1)} fusion(s32[16]{0:T(128)} %constant.414, s32[4]{0:T(128)} %param.10), kind=kLoop, calls=%fused_computation.32 | loop fusion | flops 64 | bytes 144 | tf_op jit(solution)/shard_map/eq | solution.py:150
  4.8 0.8 %dynamic-slice_bitcast_fusion.4 = (bf16[32,512]{1,0:T(8,128)(2,1)S(1)}, bf16[32,512]{1,0:T(8,128)(2,1)S(1)}, bf16[32,512]{1,0:T(8,128)(2,1)S(1)}, bf16[32,512]{1,0:T(8,128)(2,1)S(1)}) fusion(bf16[1,4,32,1024]{3,2,1,0:T(8,128)(2,1)} %param.8, s32[]{:T(128)S(6)} %add.154, s32[]{:T(128)S(6)} %select_n.264, s32[]{:T(128)S(6)} %add.156, s32[]{:T(128)S(6)} %add.155), kind=kLoop, calls=%fused_computation.14 | loop fusion | bytes 262160 | tf_op jit(solution)/shard_map/jit(_where)/broadcast_in_dim | solution.py:158
  5.6 0.0 copy-start.1
  5.6 1.9 %collective-permute-done = bf16[4,32,512]{2,1,0:T(8,128)(2,1)S(1)} collective-permute-done((bf16[4,32,512]{2,1,0:T(8,128)(2,1)S(1)}, bf16[4,32,512]{2,1,0:T(8,128)(2,1)S(1)}, u32[]{:S(2)}, u32[]{:S(2)}) %collective-permute-start) | collective-permute-done | bytes 131104 | tf_op jit(solution)/shard_map/ppermute | solution.py:21
  7.5 1.2 %add_convert_fusion = bf16[16,32,512]{2,1,0:T(8,128)(2,1)} fusion(pred[16]{0:T(512)(128)(4,1)S(1)} %get-tuple-element.28, pred[16]{0:T(512)(128)(4,1)S(1)} %get-tuple-element.29, pred[16]{0:T(512)(128)(4,1)S(1)} %get-tuple-element.27, bf16[32,512]{1,0:T(8,128)(2,1)S(1)} %get-tuple-element.24, bf16[32,512]{1,0:T(8,128)(2,1)S(1)} %get-tuple-element.25, ...), kind=kLoop, calls=%fused_computation.2 | loop fusion | flops 2621440 | bytes 786480 | tf_op jit(solution)/shard_map/convert_element_type | solution.py:164
  8.7 6.4 %all-to-all-start = ((bf16[16,32,512]{2,1,0:T(8,128)(2,1)}), bf16[16,32,512]{2,1,0:T(8,128)(2,1)S(1)}, u32[]{:S(2)}, u32[]{:S(2)}) async-start(bf16[16,32,512]{2,1,0:T(8,128)(2,1)} %add_convert_fusion), calls=%async_computation | async-start | bytes 1048576 | tf_op jit(solution)/shard_map/all_to_all | solution.py:166
  15.1 0.0 copy-done.3
  15.1 0.0 copy-done
  15.1 0.1 select_reduce_fusion
  15.2 0.6 %fusion = s32[]{:T(128)} fusion(s32[2]{0:T(128)S(1)} %select_reduce_fusion, s32[]{:T(128)S(6)} %axis_index.33), kind=kLoop, calls=%fused_computation.33 | loop fusion | flops 5 | bytes 16 | tf_op jit(solution)/shard_map/reduce_sum | solution.py:95
  17.2 0.0 copy-done.2
  17.2 1.3 %constant_dynamic-slice_fusion = (bf16[1,1,512,512]{3,2,1,0:T(8,128)(2,1)S(1)}, bf16[1,1,512,512]{3,2,1,0:T(8,128)(2,1)S(1)}) fusion(bf16[1,5,512,512]{3,2,1,0:T(8,128)(2,1)} %param.9, s32[]{:T(128)S(6)} %select_n.278), kind=kLoop, calls=%fused_computation.25 | loop fusion | bytes 2097156 | tf_op jit(solution)/shard_map/jit(dynamic_index_in_dim)/dynamic_slice | solution.py:25
  18.5 0.0 copy-start.4
  18.5 0.6 %gather_fusion = bf16[16,32,512]{2,1,0:T(8,128)(2,1)S(1)} fusion(bf16[16,32,512]{2,1,0:T(8,128)(2,1)S(1)} %bitcast.57, s32[1024]{0:T(1024)S(1)} %pad_clamp_fusion.1), kind=kCustom, calls=%fused_computation | custom fusion | bytes 1048640 | tf_op jit(solution)/shard_map/jit(_take)/gather | solution.py:45
  19.1 0.0 copy-done.1
  19.1 0.6 %gather_fusion.1 = bf16[8,64,512]{2,1,0:T(8,128)(2,1)S(1)} fusion(bf16[8,64,512]{2,1,0:T(8,128)(2,1)S(1)} %bitcast.56, s32[1024]{0:T(1024)S(1)} %pad_clamp_fusion), kind=kCustom, calls=%fused_computation.1 | custom fusion | bytes 1048608 | tf_op jit(solution)/shard_map/jit(_take)/gather | solution.py:45
  19.7 7.0 %all-to-all-done = bf16[16,32,512]{2,1,0:T(8,128)(2,1)S(1)} async-done(((bf16[16,32,512]{2,1,0:T(8,128)(2,1)}), bf16[16,32,512]{2,1,0:T(8,128)(2,1)S(1)}, u32[]{:S(2)}, u32[]{:S(2)}) %all-to-all-start) | async-done | bytes 524320 | tf_op jit(solution)/shard_map/all_to_all | solution.py:166
  26.7 1.5 %shard_map.82 = bf16[2,512,256]{2,1,0:T(8,128)(2,1)} custom-call(bf16[512,512]{1,0:T(8,128)(2,1)S(1)} %bitcast.53, bf16[512,512]{1,0:T(8,128)(2,1)S(1)} %bitcast.54, bf16[512,512]{1,0:T(8,128)(2,1)S(1)} %bitcast.55), custom_call_target="tpu_custom_call" | custom-call | flops 536870912 | bytes 2097152 | tf_op jit(solution)/shard_map/pallas_call | solution.py:73
  28.2 5.1 %all-to-all-start.1 = ((bf16[16,64,256]{2,1,0:T(8,128)(2,1)}), bf16[16,64,256]{2,1,0:T(8,128)(2,1)S(1)}, u32[]{:S(2)}, u32[]{:S(2)}) async-start(bf16[16,64,256]{2,1,0:T(8,128)(2,1)} %bitcast.21), calls=%async_computation.1 | async-start | bytes 1048576 | tf_op jit(solution)/shard_map/all_to_all | solution.py:104
  33.3 0.0 copy-done.4
  33.3 0.6 %multiply_reduce_fusion = s32[]{:T(128)} fusion(s32[4]{0:T(128)S(1)} %copy-done.3, s32[4]{0:T(128)S(1)} %copy-done.4), kind=kLoop, calls=%fused_computation.34 | loop fusion | flops 7 | bytes 36 | tf_op jit(solution)/shard_map/reduce_sum | solution.py:32
  36.9 4.7 %all-to-all-done.1 = bf16[16,64,256]{2,1,0:T(8,128)(2,1)S(1)} async-done(((bf16[16,64,256]{2,1,0:T(8,128)(2,1)}), bf16[16,64,256]{2,1,0:T(8,128)(2,1)S(1)}, u32[]{:S(2)}, u32[]{:S(2)}) %all-to-all-start.1) | async-done | bytes 524320 | tf_op jit(solution)/shard_map/all_to_all | solution.py:104
  41.7 2.7 %collective-permute-start.1 = (bf16[4,64,256]{2,1,0:T(8,128)(2,1)S(1)}, bf16[4,64,256]{2,1,0:T(8,128)(2,1)S(1)}, u32[]{:S(2)}, u32[]{:S(2)}) collective-permute-start(bf16[4,64,256]{2,1,0:T(8,128)(2,1)S(1)} %pad_maximum_fusion), channel_id=1, source_target_pairs={{0,8},{1,9},{2,10},{3,11},{4,12},{5,13},{6,14},{7,15},{8,0},{9,1},... | collective-permute-start | bytes 393224 | tf_op jit(solution)/shard_map/ppermute | solution.py:21
  44.3 0.1 pad_add_fusion
  44.4 5.1 %collective-permute-done.1 = bf16[4,64,256]{2,1,0:T(8,128)(2,1)S(1)} collective-permute-done((bf16[4,64,256]{2,1,0:T(8,128)(2,1)S(1)}, bf16[4,64,256]{2,1,0:T(8,128)(2,1)S(1)}, u32[]{:S(2)}, u32[]{:S(2)}) %collective-permute-start.1) | collective-permute-done | bytes 131104 | tf_op jit(solution)/shard_map/ppermute | solution.py:21
  49.5 0.8 %convert_bitcast_fusion = f32[4,256,64]{1,2,0:T(8,128)} fusion(bf16[4,64,256]{2,1,0:T(8,128)(2,1)S(1)} %collective-permute-done.1, bf16[1,64,256]{2,1,0:T(8,128)(2,1)S(1)} %get-tuple-element.12, bf16[1,64,256]{2,1,0:T(8,128)(2,1)S(1)} %get-tuple-element.13, bf16[1,64,256]{2,1,0:T(8,128)(2,1)S(1)} %get-tuple-element.14, ...), kind=kLoop, calls=%fused_computation.3 | loop fusion | flops 327680 | bytes 524292 | tf_op jit(solution)/shard_map/transpose | solution.py:176
  (7 shorter events, 0.1 us)
Async XLA Ops:
  0.0 17.2 %copy-start.2 = (s32[16]{0:T(128)S(1)}, s32[16]{0:T(128)}, u32[]{:S(2)}) copy-start(s32[16]{0:T(128)} %constant.414) | copy-start | bytes 196
  0.0 15.1 %copy-start.3 = (s32[4]{0:T(128)S(1)}, s32[4]{0:T(128)}, u32[]{:S(2)}) copy-start(s32[4]{0:T(128)} %param.10) | copy-start | bytes 52
  0.0 15.1 %copy-start = (s32[4,2]{0,1:T(2,128)S(1)}, s32[4,2]{0,1:T(2,128)}, u32[]{:S(2)}) copy-start(s32[4,2]{0,1:T(2,128)} %param.11) | copy-start | bytes 100
  1.0 6.5 %collective-permute-start = (bf16[4,32,512]{2,1,0:T(8,128)(2,1)S(1)}, bf16[4,32,512]{2,1,0:T(8,128)(2,1)S(1)}, u32[]{:S(2)}, u32[]{:S(2)}) collective-permute-start(bf16[4,32,512]{2,1,0:T(8,128)(2,1)S(1)} %dynamic-slice_bitcast_fusion), channel_id=1, source_target_pairs={{0,16},{16,0},{1,17},{17,1},{2,18},{18,2},{3,19},{19,3},{4,20},{20... | collective-permute-start | bytes 393224 | tf_op jit(solution)/shard_map/ppermute | solution.py:21
  5.6 13.5 %copy-start.1 = (s32[8]{0:T(128)S(1)}, s32[8]{0:T(128)}, u32[]{:S(2)}) copy-start(s32[8]{0:T(128)} %constant.432) | copy-start | bytes 100
  8.7 18.0 %all-to-all-start = ((bf16[16,32,512]{2,1,0:T(8,128)(2,1)}), bf16[16,32,512]{2,1,0:T(8,128)(2,1)S(1)}, u32[]{:S(2)}, u32[]{:S(2)}) async-start(bf16[16,32,512]{2,1,0:T(8,128)(2,1)} %add_convert_fusion), calls=%async_computation | async-start | bytes 1048576 | tf_op jit(solution)/shard_map/all_to_all | solution.py:166
  18.5 14.8 %copy-start.4 = (s32[4]{0:T(128)S(1)}, s32[4]{0:T(128)}, u32[]{:S(2)}) copy-start(s32[4]{0:T(128)} %constant.409.clone) | copy-start | bytes 52
  28.2 13.4 %all-to-all-start.1 = ((bf16[16,64,256]{2,1,0:T(8,128)(2,1)}), bf16[16,64,256]{2,1,0:T(8,128)(2,1)S(1)}, u32[]{:S(2)}, u32[]{:S(2)}) async-start(bf16[16,64,256]{2,1,0:T(8,128)(2,1)} %bitcast.21), calls=%async_computation.1 | async-start | bytes 1048576 | tf_op jit(solution)/shard_map/all_to_all | solution.py:104
  41.7 7.8 %collective-permute-start.1 = (bf16[4,64,256]{2,1,0:T(8,128)(2,1)S(1)}, bf16[4,64,256]{2,1,0:T(8,128)(2,1)S(1)}, u32[]{:S(2)}, u32[]{:S(2)}) collective-permute-start(bf16[4,64,256]{2,1,0:T(8,128)(2,1)S(1)} %pad_maximum_fusion), channel_id=1, source_target_pairs={{0,8},{1,9},{2,10},{3,11},{4,12},{5,13},{6,14},{7,15},{8,0},{9,1},... | collective-permute-start | bytes 393224 | tf_op jit(solution)/shard_map/ppermute | solution.py:21
